TPU v7x, 128 devices: a whole 4x4x4 slice. The times are simulated.
128 devices in a mesh: expert: 64 (over z, y, x), fsdp: 2 (over core).
Axes of the slice: x: 4, y: 4, z: 4, core: 2. Of those that a mesh axis runs over, the one named last changes fastest.
Arguments:
- out_grad: bfloat16 [8192, 2560], P('expert', 'fsdp'), may hold values from -6 to 6
- expert_ids: int32 [8192, 6], P('expert'), may hold values from 0 to 63, all different within a row; in each aligned block of 128 rows (0 to 127, 128 to 255, ...) at most 18 rows name the same one
- gate_probs: float32 [8192, 6], P('expert'), may hold values from 0.02 to 0.6
- saved_inputs: bfloat16 [64, 1152, 2560], P('expert', 'fsdp'), may hold values from -6 to 6
- gate_weight: bfloat16 [64, 2560, 768], P('expert', 'fsdp'), may hold values from -0.125 to 0.125
- up_weight: bfloat16 [64, 2560, 768], P('expert', 'fsdp'), may hold values from -0.125 to 0.125
- down_weight: bfloat16 [64, 2560, 768], P('expert', 'fsdp'), may hold values from -0.21875 to 0.21875
Outputs:
- input_grad: bfloat16 [8192, 2560], P('expert', 'fsdp')
- gate_grad: bfloat16 [8192, 6], P('expert')
- down_grad: float32 [64, 2560, 768], P('expert', 'fsdp')
Inputs may be any that keep to these rules, and one draw needn't show every extreme that they name: `expert_ids`: each row names 6 different experts. The rows of one block of 128 tokens name any one expert at most 18 times, and in every draw the rows of some block name some expert exactly 18 times.
All inputs are finite; a program needn't handle non-finite values.
Results may differ from a plain program's by a relative error of at most 0.011.
Values may be sent and summed in bfloat16 or wider, within the bound.
A program may use at most 128 MiB of HBM per device.

v0:
```python
import jax
import jax.numpy as jnp
from jax import lax
from jax.sharding import PartitionSpec as P


def body(out_grad, expert_ids, gate_probs, saved_inputs, gate_weight, up_weight, down_weight):
    tok_rows, shard_width = out_grad.shape
    top_count = expert_ids.shape[1]
    senders = lax.axis_size("expert")
    groups = lax.axis_size("fsdp")
    local_rows = saved_inputs.shape[1]
    slot_count = local_rows * groups
    slot_depth = slot_count // senders
    routes = tok_rows * top_count
    flat_ids = expert_ids.reshape(routes)
    route_table = (flat_ids[:, None] == jnp.arange(senders, dtype=jnp.int32)[None, :]).astype(
        jnp.int32
    )
    earlier = jnp.cumsum(route_table, axis=0) - route_table
    route_rank = jnp.sum(earlier * route_table, axis=1)
    slot_of = flat_ids * slot_depth + route_rank
    placed = slot_of[:, None] == jnp.arange(slot_count, dtype=jnp.int32)[None, :]
    placed_float = placed.astype(jnp.float32)
    token_slots = jnp.any(placed.reshape(tok_rows, top_count, slot_count), axis=1).astype(
        jnp.bfloat16
    )
    send_rows = lax.dot_general(
        token_slots, out_grad, (((0,), (0,)), ((), ())), preferred_element_type=jnp.float32
    ).astype(jnp.bfloat16)
    send_prob = jnp.dot(
        gate_probs.reshape(routes), placed_float, precision=lax.Precision.HIGHEST
    ).astype(jnp.bfloat16)
    grad_feat, prob_half = (
        lax.all_to_all(send_rows, "expert", split_axis=0, concat_axis=0, tiled=True),
        lax.all_to_all(send_prob, "expert", split_axis=0, concat_axis=0, tiled=True),
    )
    prob_all = prob_half.astype(jnp.float32)
    row_begin = lax.axis_index("fsdp") * local_rows
    prob_local = lax.dynamic_slice_in_dim(prob_all, row_begin, local_rows)
    inputs = saved_inputs[0]
    gate_full, up_full = (
        lax.all_gather(gate_weight[0], "fsdp", axis=0, tiled=True),
        lax.all_gather(up_weight[0], "fsdp", axis=0, tiled=True),
    )
    down_shard = down_weight[0]
    picked = grad_feat
    raw_grad = lax.psum_scatter(
        jnp.dot(picked, down_shard, preferred_element_type=jnp.float32),
        "fsdp",
        scatter_dimension=0,
        tiled=True,
    )
    gate_pre = jnp.dot(inputs, gate_full, preferred_element_type=jnp.float32)
    up_pre = jnp.dot(inputs, up_full, preferred_element_type=jnp.float32)
    hidden = (jax.nn.silu(gate_pre) * up_pre).astype(jnp.bfloat16)
    slot_gate = jnp.sum(raw_grad * hidden.astype(jnp.float32), axis=1).astype(jnp.bfloat16)
    scaled_grad = (prob_all[:, None] * grad_feat.astype(jnp.float32)).astype(jnp.bfloat16)
    hidden_grad = prob_local[:, None] * raw_grad
    sigmoid_gate = jax.nn.sigmoid(gate_pre)
    gate_pre_grad = (
        hidden_grad * up_pre * sigmoid_gate * (1.0 + gate_pre * (1.0 - sigmoid_gate))
    ).astype(jnp.bfloat16)
    up_pre_grad = (hidden_grad * jax.nn.silu(gate_pre)).astype(jnp.bfloat16)
    contract_hidden = (((1,), (1,)), ((), ()))
    slot_input = (
        lax.dot_general(
            gate_pre_grad, gate_full, contract_hidden, preferred_element_type=jnp.float32
        )
        + lax.dot_general(up_pre_grad, up_full, contract_hidden, preferred_element_type=jnp.float32)
    ).astype(jnp.bfloat16)
    picked = scaled_grad
    down_grad = lax.dot_general(
        picked,
        lax.all_gather(hidden, "fsdp", axis=0, tiled=True),
        (((0,), (0,)), ((), ())),
        preferred_element_type=jnp.float32,
    )
    gate_copies = jnp.broadcast_to(slot_gate[:, None], (local_rows, groups))
    back_feat, back_gate = (
        lax.all_to_all(slot_input, "fsdp", split_axis=1, concat_axis=0, tiled=True),
        lax.all_to_all(gate_copies, "fsdp", split_axis=1, concat_axis=0, tiled=True),
    )
    home_rows, home_gate = (
        lax.all_to_all(back_feat, "expert", split_axis=0, concat_axis=0, tiled=True),
        lax.all_to_all(back_gate, "expert", split_axis=0, concat_axis=0, tiled=True),
    )
    input_grad = jnp.dot(token_slots, home_rows, preferred_element_type=jnp.float32).astype(
        jnp.bfloat16
    )
    gate_grad = (
        jnp.dot(
            placed_float,
            home_gate.reshape(slot_count).astype(jnp.float32),
            precision=lax.Precision.HIGHEST,
        )
        .reshape(tok_rows, top_count)
        .astype(jnp.bfloat16)
    )
    return (input_grad, gate_grad, down_grad[None])


def solution(mesh):
    placed = (
        P("expert", "fsdp"),
        P("expert", None),
        P("expert", None),
        P("expert", "fsdp", None),
        P("expert", "fsdp", None),
        P("expert", "fsdp", None),
        P("expert", "fsdp", None),
    )
    return jax.shard_map(
        body,
        mesh=mesh,
        in_specs=placed,
        out_specs=(P("expert", "fsdp"), P("expert", None), P("expert", "fsdp", None)),
        check_vma=False,
    )
```

profile of v0, /device:TPU:1, one launch (start us, length us, event | category | flops | bytes accessed | tf_op | source)
XLA Modules:
  0.0 228.4 jit_solution(14098937664145165270)
XLA Ops:
  7.2 0.7 all-gather.10.cloned.1.call-update
  8.0 0.7 all-gather.8.cloned.1.call-update
  9.1 1.8 reduce-window.6
  12.2 3.5 %convolution_convert_fusion = bf16[1152,1280]{1,0:T(8,128)(2,1)} fusion(pred[128,1152]{1,0:T(8,128)(4,1)S(1)} %fusion.7, bf16[128,1280]{1,0:T(8,128)(2,1)} %param.7), kind=kOutput, calls=%fused_computation | convolution fusion | flops 378961920 | bytes 3424256 | tf_op jit(solution)/shard_map/dot_general | solution.py:28
  15.7 5.4 %all_to_all.52 = bf16[64,18,1280]{2,1,0:T(8,128)(2,1)} reshape(bf16[1152,1280]{1,0:T(8,128)(2,1)} %convolution_convert_fusion) | data formatting | bytes 5898240 | tf_op jit(solution)/shard_map/all_to_all | solution.py:35
  21.2 60.4 %all_to_all.73 = bf16[64,18,1280]{2,1,0:T(8,128)(2,1)} all-to-all(bf16[64,18,1280]{2,1,0:T(8,128)(2,1)} %all_to_all.52), channel_id=1, replica_groups=mesh['expert'=64,'fsdp'=2] {'expert'}, dimensions={0} | all-to-all | bytes 5898240 | tf_op jit(solution)/shard_map/all_to_all | solution.py:35
  81.5 5.5 %all_to_all.54 = bf16[1152,1280]{1,0:T(8,128)(2,1)} reshape(bf16[64,18,1280]{2,1,0:T(8,128)(2,1)} %all_to_all.73) | data formatting | bytes 5898240 | tf_op jit(solution)/shard_map/all_to_all | solution.py:35
  87.1 6.7 %fusion.15 = f32[1152,768]{1,0:T(8,128)} fusion(bf16[1152,1280]{1,0:T(8,128)(2,1)} %all_to_all.54, bf16[1,1280,768]{2,1,0:T(8,128)(2,1)} %param.13), kind=kOutput, calls=%fused_computation.23 | convolution fusion | flops 2264924160 | bytes 8454144 | tf_op jit(solution)/shard_map/dot_general | solution.py:49
  94.7 1.3 fusion.20
  96.0 0.8 all_to_all.65
  96.8 7.0 %all-to-all-start = ((bf16[64,18,1]{1,2,0:T(2,128)(2,1)}), bf16[64,18,1]{1,2,0:T(2,128)(2,1)S(1)}, u32[]{:S(2)}, u32[]{:S(2)}) async-start(bf16[64,18,1]{1,2,0:T(2,128)(2,1)} %all_to_all.65), calls=%async_computation | async-start | bytes 65536 | tf_op jit(solution)/shard_map/all_to_all | solution.py:36
  103.8 8.1 %all-to-all-done = bf16[64,18,1]{1,2,0:T(2,128)(2,1)S(1)} async-done(((bf16[64,18,1]{1,2,0:T(2,128)(2,1)}), bf16[64,18,1]{1,2,0:T(2,128)(2,1)S(1)}, u32[]{:S(2)}, u32[]{:S(2)}) %all-to-all-start) | async-done | bytes 2336 | tf_op jit(solution)/shard_map/all_to_all | solution.py:36
  112.3 5.8 %fusion.2 = f32[576,768]{1,0:T(8,128)} fusion(bf16[1,2560,768]{2,1,0:T(8,128)(2,1)} %all-gather.10.cloned.1.call-done, bf16[1,576,2560]{2,1,0:T(8,128)(2,1)S(1)} %copy-done), kind=kOutput, calls=%fused_computation.5 | convolution fusion | flops 2264924160 | bytes 8650752 | tf_op jit(solution)/shard_map/dot_general | solution.py:54
  118.1 6.9 %multiply_reduce_fusion = (bf16[576]{0:T(1024)(128)(2,1)S(1)}, bf16[576,768]{1,0:T(8,128)(2,1)}, f32[576,768]{1,0:T(8,128)S(1)}) fusion(f32[576,768]{1,0:T(8,128)} %reduce-scatter.2.cloned.1.call-done, f32[576,768]{1,0:T(8,128)} %fusion.2, bf16[1,2560,768]{2,1,0:T(8,128)(2,1)} %all-gather.8.cloned.1.call-done, bf16[1,576,2560]{2,1,0:T(8,128)(2,1)S(1)} %copy-done), kind=kOutput, calls=%fused_computation.25 | convolution fusion | flops 2268904960 | bytes 13075584 | tf_op jit(solution)/shard_map/dot_general | solution.py:55
  125.0 3.0 %fusion = f32[576,2560]{1,0:T(8,128)S(1)} fusion(bf16[1,2560,768]{2,1,0:T(8,128)(2,1)S(1)} %copy-done.5, f32[576,768]{1,0:T(8,128)S(1)} %copy-done.8, f32[576,768]{1,0:T(8,128)S(1)} %get-tuple-element.5, f32[576,768]{1,0:T(8,128)S(1)} %copy-done.7, f32[576]{0:T(1024)S(1)} %dynamic_slice.3), kind=kOutput, calls=%fused_computation.3 | convolution fusion | flops 2269790208 | bytes 15141120 | tf_op jit(solution)/shard_map/dot_general | solution.py:67
  128.0 2.8 %add_convert_fusion = bf16[576,2560]{1,0:T(8,128)(2,1)S(1)} fusion(f32[576,2560]{1,0:T(8,128)S(1)} %fusion, bf16[1,2560,768]{2,1,0:T(8,128)(2,1)S(1)} %copy-done.6, f32[576,768]{1,0:T(8,128)S(1)} %copy-done.7, f32[576]{0:T(1024)S(1)} %dynamic_slice.3, f32[576,768]{1,0:T(8,128)S(1)} %copy-done.8), kind=kOutput, calls=%fused_computation.2 | convolution fusion | flops 2270969856 | bytes 16320768 | tf_op jit(solution)/shard_map/dot_general | solution.py:70
  130.8 1.8 copy.54
  133.9 5.6 %all_to_all.74 = bf16[2,2,288]{2,1,0:T(2,128)(2,1)S(1)} all-to-all(bf16[2,2,288]{2,1,0:T(2,128)(2,1)S(1)} %reshape.128), channel_id=1, replica_groups=mesh['expert'=64,'fsdp'=2] {'fsdp'}, dimensions={0} | all-to-all | bytes 4608 | tf_op jit(solution)/shard_map/all_to_all | solution.py:82
  139.5 4.2 %all-to-all-start.2 = ((bf16[576,2,1280]{2,0,1:T(8,128)(2,1)}), bf16[576,2,1280]{2,0,1:T(8,128)(2,1)S(1)}, u32[]{:S(2)}, u32[]{:S(2)}) async-start(bf16[576,2,1280]{2,0,1:T(8,128)(2,1)} %bitcast.67), calls=%async_computation.3 | async-start | bytes 5898240 | tf_op jit(solution)/shard_map/all_to_all | solution.py:81
  143.8 0.7 all_to_all.66
  144.6 2.2 all-to-all-done.2
  146.8 4.7 %all-to-all-start.5 = ((bf16[64,18,1]{1,2,0:T(2,128)(2,1)}), bf16[64,18,1]{1,2,0:T(2,128)(2,1)S(1)}, u32[]{:S(2)}, u32[]{:S(2)}) async-start(bf16[64,18,1]{1,2,0:T(2,128)(2,1)} %all_to_all.66), calls=%async_computation.6 | async-start | bytes 65536 | tf_op jit(solution)/shard_map/all_to_all | solution.py:86
  151.5 2.8 %all_to_all.58 = bf16[64,18,1280]{2,1,0:T(8,128)(2,1)} reshape(bf16[2,576,1280]{2,1,0:T(8,128)(2,1)S(1)} %bitcast.69) | data formatting | bytes 5898240 | tf_op jit(solution)/shard_map/all_to_all | solution.py:85
  154.3 5.6 %all-to-all-done.5 = bf16[64,18,1]{1,2,0:T(2,128)(2,1)S(1)} async-done(((bf16[64,18,1]{1,2,0:T(2,128)(2,1)}), bf16[64,18,1]{1,2,0:T(2,128)(2,1)S(1)}, u32[]{:S(2)}, u32[]{:S(2)}) %all-to-all-start.5) | async-done | bytes 2336 | tf_op jit(solution)/shard_map/all_to_all | solution.py:86
  159.9 5.6 %all-to-all-start.3 = ((bf16[64,18,1280]{2,1,0:T(8,128)(2,1)}), bf16[64,18,1280]{2,1,0:T(8,128)(2,1)}, u32[]{:S(2)}, u32[]{:S(2)}) async-start(bf16[64,18,1280]{2,1,0:T(8,128)(2,1)} %all_to_all.58), calls=%async_computation.4 | async-start | bytes 7864320 | tf_op jit(solution)/shard_map/all_to_all | solution.py:85
  166.3 0.8 fusion.9
  167.1 0.7 copy.49
  167.8 15.6 %all-gather.6.cloned.1.call-done = bf16[1152,768]{1,0:T(8,128)(2,1)} async-done(((bf16[576,768]{1,0:T(8,128)(2,1)}), bf16[1152,768]{1,0:T(8,128)(2,1)}) %all-gather.6.cloned.1.call-update) | async-done | bytes 1769488 | tf_op jit(solution)/shard_map/all_gather | solution.py:75
  183.4 6.3 %convolution_bitcast_fusion = f32[1,1280,768]{2,1,0:T(8,128)} fusion(bf16[1152,768]{1,0:T(8,128)(2,1)} %all-gather.6.cloned.1.call-done, bf16[1152,1280]{1,0:T(8,128)(2,1)S(1)} %copy-done.2, f32[1152]{0:T(1024)S(1)} %reshape.108), kind=kOutput, calls=%fused_computation.10 | convolution fusion | flops 2269347840 | bytes 8655360 | tf_op jit(solution)/shard_map/dot_general | solution.py:73
  189.7 23.3 %all-to-all-done.3 = bf16[64,18,1280]{2,1,0:T(8,128)(2,1)} async-done(((bf16[64,18,1280]{2,1,0:T(8,128)(2,1)}), bf16[64,18,1280]{2,1,0:T(8,128)(2,1)}, u32[]{:S(2)}, u32[]{:S(2)}) %all-to-all-start.3) | async-done | bytes 2949152 | tf_op jit(solution)/shard_map/all_to_all | solution.py:85
  213.0 5.7 %all_to_all.60 = bf16[1152,1280]{1,0:T(8,128)(2,1)} reshape(bf16[64,18,1280]{2,1,0:T(8,128)(2,1)} %all-to-all-done.3) | data formatting | bytes 5898240 | tf_op jit(solution)/shard_map/all_to_all | solution.py:85
  218.7 3.2 %convolution_convert_fusion.1 = bf16[128,1280]{1,0:T(8,128)(2,1)} fusion(pred[128,1152]{1,0:T(8,128)(4,1)S(1)} %fusion.7, bf16[1152,1280]{1,0:T(8,128)(2,1)} %all_to_all.60), kind=kOutput, calls=%fused_computation.22 | convolution fusion | flops 377651200 | bytes 3424256 | tf_op jit(solution)/shard_map/dot_general | solution.py:88
  (52 shorter events, 5.2 us)
Async XLA Ops:
  7.2 105.1 %copy-start = (bf16[1,576,2560]{2,1,0:T(8,128)(2,1)S(1)}, bf16[1,576,2560]{2,1,0:T(8,128)(2,1)}, u32[]{:S(2)}) copy-start(bf16[1,576,2560]{2,1,0:T(8,128)(2,1)} %param.10) | copy-start | bytes 8847364
  7.2 1.5 copy-start.3
  7.2 105.1 %all-gather.10.cloned.1.call-start = ((), (), s32[]{:S(2)}) async-start(), calls=%async_computation.10 | async-start | bytes 5898240 | tf_op jit(solution)/shard_map/all_gather | solution.py:43
  7.9 110.2 %all-gather.8.cloned.1.call-start = ((), (), s32[]{:S(2)}) async-start(), calls=%async_computation.9 | async-start | bytes 5898240 | tf_op jit(solution)/shard_map/all_gather | solution.py:44
  8.7 109.4 %reduce-scatter.2.cloned.1.call-start = ((), (), s32[]{:S(2)}) async-start(), calls=%async_computation.7 | async-start | bytes 5308416 | tf_op jit(solution)/shard_map/reduce_scatter | solution.py:48
  93.8 0.7 copy-start.4
  96.8 15.2 %all-to-all-start = ((bf16[64,18,1]{1,2,0:T(2,128)(2,1)}), bf16[64,18,1]{1,2,0:T(2,128)(2,1)S(1)}, u32[]{:S(2)}, u32[]{:S(2)}) async-start(bf16[64,18,1]{1,2,0:T(2,128)(2,1)} %all_to_all.65), calls=%async_computation | async-start | bytes 65536 | tf_op jit(solution)/shard_map/all_to_all | solution.py:36
  118.1 6.9 %copy-start.5 = (bf16[1,2560,768]{2,1,0:T(8,128)(2,1)S(1)}, bf16[1,2560,768]{2,1,0:T(8,128)(2,1)}, u32[]{:S(2)}) copy-start(bf16[1,2560,768]{2,1,0:T(8,128)(2,1)} %all-gather.10.cloned.1.call-done) | copy-start | bytes 11796484
  118.1 6.9 %copy-start.7 = (f32[576,768]{1,0:T(8,128)S(1)}, f32[576,768]{1,0:T(8,128)}, u32[]{:S(2)}) copy-start(f32[576,768]{1,0:T(8,128)} %reduce-scatter.2.cloned.1.call-done) | copy-start | bytes 5308420
  118.1 6.9 %copy-start.8 = (f32[576,768]{1,0:T(8,128)S(1)}, f32[576,768]{1,0:T(8,128)}, u32[]{:S(2)}) copy-start(f32[576,768]{1,0:T(8,128)} %fusion.2) | copy-start | bytes 5308420
  125.0 3.0 %copy-start.6 = (bf16[1,2560,768]{2,1,0:T(8,128)(2,1)S(1)}, bf16[1,2560,768]{2,1,0:T(8,128)(2,1)}, u32[]{:S(2)}) copy-start(bf16[1,2560,768]{2,1,0:T(8,128)(2,1)} %all-gather.8.cloned.1.call-done) | copy-start | bytes 11796484
  139.5 7.3 %all-to-all-start.2 = ((bf16[576,2,1280]{2,0,1:T(8,128)(2,1)}), bf16[576,2,1280]{2,0,1:T(8,128)(2,1)S(1)}, u32[]{:S(2)}, u32[]{:S(2)}) async-start(bf16[576,2,1280]{2,0,1:T(8,128)(2,1)} %bitcast.67), calls=%async_computation.3 | async-start | bytes 5898240 | tf_op jit(solution)/shard_map/all_to_all | solution.py:81
  146.8 13.0 %all-to-all-start.5 = ((bf16[64,18,1]{1,2,0:T(2,128)(2,1)}), bf16[64,18,1]{1,2,0:T(2,128)(2,1)S(1)}, u32[]{:S(2)}, u32[]{:S(2)}) async-start(bf16[64,18,1]{1,2,0:T(2,128)(2,1)} %all_to_all.66), calls=%async_computation.6 | async-start | bytes 65536 | tf_op jit(solution)/shard_map/all_to_all | solution.py:86
  154.3 29.1 %copy-start.2 = (bf16[1152,1280]{1,0:T(8,128)(2,1)S(1)}, bf16[1152,1280]{1,0:T(8,128)(2,1)}, u32[]{:S(2)}) copy-start(bf16[1152,1280]{1,0:T(8,128)(2,1)} %all_to_all.54) | copy-start | bytes 8847364
  159.9 53.1 %all-to-all-start.3 = ((bf16[64,18,1280]{2,1,0:T(8,128)(2,1)}), bf16[64,18,1280]{2,1,0:T(8,128)(2,1)}, u32[]{:S(2)}, u32[]{:S(2)}) async-start(bf16[64,18,1280]{2,1,0:T(8,128)(2,1)} %all_to_all.58), calls=%async_computation.4 | async-start | bytes 7864320 | tf_op jit(solution)/shard_map/all_to_all | solution.py:85
  165.5 17.9 %all-gather.6.cloned.1.call-start = ((), (), s32[]{:S(2)}) async-start(), calls=%async_computation.8 | async-start | bytes 2654208 | tf_op jit(solution)/shard_map/all_gather | solution.py:75
  213.0 8.9 %copy-start.1 = (bf16[1,576,2560]{2,1,0:T(8,128)(2,1)S(1)}, bf16[1,576,2560]{2,1,0:T(8,128)(2,1)}, u32[]{:S(2)}) copy-start(bf16[1,576,2560]{2,1,0:T(8,128)(2,1)} %param.10) | copy-start | bytes 8847364
Sparse Core Ops, SparseCore 0:
  9.7 19.6 all-gather.9
  31.0 17.3 all-gather.7
  93.9 12.5 reduce-scatter.1
  167.8 15.5 all-gather.5
where the time goes:
time: 232 us; the launch traced here: 228 us
  blocking collectives  65.9 us (28%)
  waiting for transfers between devices  56.5 us (24%)
  matrix products  40.2 us (17%)
  local copies, waits for them, and re-layouts  26.4 us (11%)
  starting transfers between devices  21.9 us (9%)
  between operations  14 us (6%)
  other arithmetic  3.44 us (1%)
    all_to_all x1, blocking collectives, body(): lax.all_to_all(send_rows, 'expert', split_axis=0, concat_axis=0, tiled=True)  60.4 us
    all_to_all x1, waiting for transfers between devices, body(): lax.all_to_all(back_feat, 'expert', split_axis=0, concat_axis=0, tiled=True)  23.3 us
    all_gather x1, waiting for transfers between devices, body(): lax.all_gather(hidden, 'fsdp', axis=0, tiled=True)  15.6 us
    all_to_all x2, local copies, waits for them, and re-layouts, body(): lax.all_to_all(send_rows, 'expert', split_axis=0, concat_axis=0, tiled=True)  11 us
    all_to_all x2, local copies, waits for them, and re-layouts, body(): lax.all_to_all(back_feat, 'expert', split_axis=0, concat_axis=0, tiled=True)  8.46 us
    all_to_all x1, waiting for transfers between devices, body(): lax.all_to_all(send_prob, 'expert', split_axis=0, concat_axis=0, tiled=True)  8.15 us
    all_to_all x1, starting transfers between devices, body(): lax.all_to_all(send_prob, 'expert', split_axis=0, concat_axis=0, tiled=True)  7.03 us
    dot_general x1, matrix products, body(): up_pre = jnp.dot(inputs, up_full, preferred_element_type=jnp.float32)  6.92 us
  transfers between devices with their start and end apart: 8, of which 5 were waited for; matrix products, arithmetic and copies ran while one was open for 13% of the time, Pallas kernels for 0%

commit v1 on v0

v1 whole, which is shorter than its diff:
```python
import functools

import jax
import jax.numpy as jnp
from jax import lax
from jax.experimental import pallas as pl
from jax.experimental.pallas import tpu as pltpu
from jax.sharding import PartitionSpec as P

MESH = pl.DeviceIdType.MESH
F32 = jnp.float32
BF16 = jnp.bfloat16
E = 64
PL = 16
CAP = 18
MAIN = 16
G = PL * CAP


def iota(shape, dim):
    return lax.broadcasted_iota(jnp.int32, shape, dim)


def target(me, o):
    z, y, x = me // 16, (me // 4) % 4, me % 4
    return ((z + o // 16) % 4) * 16 + ((y + (o // 4) % 4) % 4) * 4 + (x + o % 4) % 4


def kernel(
    ids_ref, prob_ref, og_ref, sin_hbm, gw_hbm, uw_hbm, dw_hbm,
    ig_ref, gg_ref, dg_hbm,
    msg, recv, xs, scr, sin, xin, wg, wu, wd, bm, cm, hid, pown, psend, precv, gpg, upg,
    msg2, rec2, wmain, wovf, gm, acc, dgv, sref, stref, ptref,
    lsem, wsem, hsem, psem, ssem, rsem, ssem2, rsem2, dsem,
):
    me = lax.axis_index("expert")
    f = lax.axis_index("fsdp")
    z = me // PL
    feat = og_ref.shape[1]
    tiles = feat // 128

    loads = [
        pltpu.make_async_copy(dw_hbm.at[0], wd, lsem.at[0]),
        pltpu.make_async_copy(sin_hbm.at[0], sin, lsem.at[1]),
        pltpu.make_async_copy(gw_hbm.at[0], wg.at[f], lsem.at[2]),
        pltpu.make_async_copy(uw_hbm.at[0], wu.at[f], lsem.at[3]),
    ]
    for c in loads[1:] + loads[:1]:
        c.start()

    barrier = pltpu.get_barrier_semaphore()

    def greet(i, carry):
        d = target(me, i)
        pl.semaphore_signal(barrier, inc=1, device_id=(d, f), device_id_type=MESH)
        pl.semaphore_signal(barrier, inc=1, device_id=(d, 1 - f), device_id_type=MESH)
        return carry

    pl.semaphore_signal(barrier, inc=1, device_id=(me, 1 - f), device_id_type=MESH)
    lax.fori_loop(1, E, greet, 0)

    lane = iota((128, 128), 1)
    row = iota((128, 128), 0)
    names = jnp.zeros((128, 128), F32)
    probs = jnp.zeros((128, 128), F32)
    for k in range(ids_ref.shape[1]):
        hit = ids_ref[:, k : k + 1] == lane
        names = names + hit.astype(F32)
        probs = probs + jnp.where(hit, prob_ref[:, k : k + 1], 0.0)
    before = (lane < row).astype(BF16)
    rank = jnp.dot(before, names.astype(BF16), preferred_element_type=F32)
    s = jnp.where(names > 0.0, rank, -1.0)
    sref[...] = s
    stref[...] = s.T
    ptref[...] = probs.astype(BF16).astype(F32).T

    st_half, pt_half = stref[...].astype(BF16), ptref[...].astype(BF16)

    def rows_of(g, carry):
        r = iota((256, 128), 0)
        spread = (r // MAIN + PL * g == iota((256, 128), 1)).astype(BF16)
        s_rep = jnp.dot(spread, st_half, preferred_element_type=F32)
        p_rep = jnp.dot(spread, pt_half, preferred_element_type=F32)
        lhs = jnp.where(s_rep == (r % MAIN).astype(F32), p_rep, 0.0).astype(BF16)
        rows = jnp.dot(lhs, og_ref[...], preferred_element_type=F32).astype(BF16)
        msg[pl.ds(PL * g, PL), :, 0:feat] = rows.reshape(PL, MAIN, feat)
        return carry

    lax.fori_loop(0, 4, rows_of, 0)
    scr[...] = jnp.zeros_like(scr)
    for c in range(CAP - MAIN):
        lhs = jnp.where(stref[0:E, :] == float(MAIN + c), ptref[0:E, :], 0.0).astype(BF16)
        rows = jnp.dot(lhs, og_ref[...], preferred_element_type=F32)
        for j in range(tiles):
            scr[pl.ds(c * tiles + j, E, stride=32), :] = rows[:, 128 * j : 128 * (j + 1)]
    packed = scr[...].reshape(E, 32, 128).astype(BF16)
    msg[:, :, feat : feat + 128] = packed[:, 0:16, :]
    msg[:, :, feat + 128 : feat + 256] = packed[:, 16:32, :]

    pl.semaphore_wait(barrier, 2 * (E - 1) + 1)

    def weight_copies():
        return [
            pltpu.make_async_remote_copy(
                src_ref=h.at[0], dst_ref=w.at[f], send_sem=wsem.at[0, i], recv_sem=wsem.at[1, i],
                device_id=(me, 1 - f), device_id_type=MESH,
            )
            for i, (h, w) in enumerate(((gw_hbm, wg), (uw_hbm, wu)))
        ]

    for c in weight_copies():
        c.start()

    def dispatch(i, carry):
        d = target(me, (i * 23) % E)
        pltpu.make_async_remote_copy(
            src_ref=msg.at[d], dst_ref=recv.at[me], send_sem=ssem.at[0], recv_sem=rsem.at[z],
            device_id=(d, f), device_id_type=MESH,
        ).start()
        return carry

    lax.fori_loop(1, E, dispatch, 0)
    pltpu.make_async_copy(msg.at[me], recv.at[me], rsem.at[z]).start()

    s_half = sref[...].astype(BF16)
    for g in range(4):
        r = iota((128, 256), 1)
        spread = (r // MAIN + PL * g == iota((128, 256), 0)).astype(BF16)
        s_rep = jnp.dot(s_half, spread, preferred_element_type=F32)
        wmain[g] = (s_rep == (r % MAIN).astype(F32)).astype(BF16)
        r = iota((128, 32), 1)
        spread = (r % PL + PL * g == iota((128, 32), 0)).astype(BF16)
        s_rep = jnp.dot(s_half, spread, preferred_element_type=F32)
        wovf[g] = (s_rep == (MAIN + r // PL).astype(F32)).astype(BF16)

    loads[1].wait()
    r = iota((G, G), 0)
    origin = jnp.where(
        r < PL * MAIN, CAP * (r // MAIN) + r % MAIN,
        CAP * ((r - PL * MAIN) % PL) + MAIN + (r - PL * MAIN) // PL,
    )
    perm = (origin == iota((G, G), 1)).astype(BF16)
    for q in range(2):
        for n in range(0, 2 * feat, 512):
            xin[q, :, n : n + 512] = jnp.dot(
                perm, sin[G * q : G * (q + 1), n : n + 512], preferred_element_type=F32
            ).astype(BF16)

    loads[2].wait()
    loads[3].wait()
    for c in weight_copies():
        c.wait()
    for n in range(0, wd.shape[1], 256):
        cols = slice(n, n + 256)

        def gated(q, carry):
            a, b = xin[q, :, 0:feat], xin[q, :, feat : 2 * feat]
            gate = jnp.dot(a, wg[0, :, cols], preferred_element_type=F32) + jnp.dot(
                b, wg[1, :, cols], preferred_element_type=F32
            )
            up = jnp.dot(a, wu[0, :, cols], preferred_element_type=F32) + jnp.dot(
                b, wu[1, :, cols], preferred_element_type=F32
            )
            sg = jax.nn.sigmoid(gate)
            silu = gate * sg
            cm[q, :, cols] = silu
            bm[q, :, cols] = up * sg * (1.0 + gate * (1.0 - sg))
            hid[f, q, :, cols] = (silu * up).astype(BF16)
            return carry

        lax.fori_loop(0, 2, gated, 0)

    hid_copy = pltpu.make_async_remote_copy(
        src_ref=hid.at[f], dst_ref=hid.at[f], send_sem=hsem.at[0], recv_sem=hsem.at[1],
        device_id=(me, 1 - f), device_id_type=MESH,
    )
    hid_copy.start()

    def overflow_rows(ref, g):
        tail = ref[pl.ds(PL * g, PL), :, feat : feat + 256].astype(F32)
        for h in range(2):
            scr[pl.ds(PL * MAIN * h, PL * MAIN), :] = tail[:, :, 128 * h : 128 * (h + 1)].reshape(
                PL * MAIN, 128
            )

        def piece(i):
            return scr[pl.ds(PL * MAIN * (i // MAIN) + i % MAIN, PL, stride=MAIN), :]

        return [
            jnp.concatenate([piece(c * tiles + j) for j in range(tiles)], axis=1) for c in range(CAP - MAIN)
        ], piece

    def unpack(i, carry):
        g = (z + i) % 4
        slab = recv.at[pl.ds(PL * g, PL)]
        pltpu.make_async_copy(slab, slab, rsem.at[g]).wait()
        xs[g, 0 : PL * MAIN, :] = recv[pl.ds(PL * g, PL), :, 0:feat].reshape(PL * MAIN, feat)
        ovf, _ = overflow_rows(recv, g)
        xs[g, PL * MAIN : G, :] = jnp.concatenate(ovf, axis=0).astype(BF16)
        return carry

    lax.fori_loop(0, 4, unpack, 0)
    loads[0].wait()

    def partial_copy(q):
        return pltpu.make_async_remote_copy(
            src_ref=psend.at[q], dst_ref=precv.at[q], send_sem=psem.at[0, q], recv_sem=psem.at[1, q],
            device_id=(me, 1 - f), device_id_type=MESH,
        )

    def other(q, carry):
        psend[q] = jnp.dot(xs[2 * (1 - f) + q], wd[...], preferred_element_type=F32)
        partial_copy(q).start()
        return carry

    lax.fori_loop(0, 2, other, 0)

    def own(q, carry):
        pown[q] = jnp.dot(xs[2 * f + q], wd[...], preferred_element_type=F32)
        return carry

    lax.fori_loop(0, 2, own, 0)

    def back(i, carry):
        q = (i + z) % 2
        partial_copy(q).wait_recv()
        raw = pown[q] + precv[q]
        gpg[...] = (raw * bm[q]).astype(BF16)
        upg[...] = (raw * cm[q]).astype(BF16)
        gates = jnp.sum(raw * hid[f, q].astype(F32), axis=1, keepdims=True)
        r, ln = iota((PL * MAIN, 128), 0), iota((PL * MAIN, 128), 1)
        table = jnp.where(ln == r % MAIN, gates[0 : PL * MAIN], 0.0).reshape(PL, MAIN, 128).sum(axis=1)
        r, ln = iota((G - PL * MAIN, 128), 0), iota((G - PL * MAIN, 128), 1)
        table = table + jnp.where(ln == MAIN + r // PL, gates[PL * MAIN : G], 0.0).reshape(
            CAP - MAIN, PL, 128
        ).sum(axis=0)
        for h in range(2):
            out = msg2.at[q, h]
            for n in range(0, feat, 256):
                rows = lax.dot_general(
                    gpg[...], wg[h, n : n + 256, :], (((1,), (1,)), ((), ())), preferred_element_type=F32
                ) + lax.dot_general(
                    upg[...], wu[h, n : n + 256, :], (((1,), (1,)), ((), ())), preferred_element_type=F32
                )
                out[:, :, n : n + 256] = rows[0 : PL * MAIN].astype(BF16).reshape(PL, MAIN, 256)
                for c in range(CAP - MAIN):
                    for jj in range(2):
                        scr[pl.ds(c * tiles + n // 128 + jj, PL, stride=32), :] = rows[
                            PL * (MAIN + c) : PL * (MAIN + c + 1), 128 * jj : 128 * (jj + 1)
                        ]
            scr[pl.ds(2 * tiles, PL, stride=32), :] = table
            packed = scr[0 : PL * 32, :].reshape(PL, 32, 128).astype(BF16)
            out[:, :, feat : feat + 128] = packed[:, 0:16, :]
            out[:, :, feat + 128 : feat + 256] = packed[:, 16:32, :]

            def send(j, carry):
                blk = PL * (2 * f + q) + (me % PL + 7 * j) % PL
                here = jnp.logical_and(blk == me, h == f)

                @pl.when(here)
                def _():
                    pltpu.make_async_copy(out.at[blk % PL], rec2.at[me], rsem2.at[z]).start()

                @pl.when(jnp.logical_not(here))
                def _():
                    pltpu.make_async_remote_copy(
                        src_ref=out.at[blk % PL], dst_ref=rec2.at[me], send_sem=ssem2.at[q, h],
                        recv_sem=rsem2.at[z], device_id=(blk, h), device_id_type=MESH,
                    ).start()

                return carry

            lax.fori_loop(0, PL, send, 0)
        return carry

    lax.fori_loop(0, 2, back, 0)

    hid_copy.wait()
    inner = hid.shape[3]

    def down(m, carry):
        at = pl.multiple_of(m * 256, 256)
        lhs = xs[:, :, pl.ds(at, 256)].reshape(4 * G, 256)
        dgv[m] = lax.dot_general(
            lhs, hid[...].reshape(4 * G, inner), (((0,), (0,)), ((), ())), preferred_element_type=F32
        )
        pltpu.make_async_copy(dgv.at[m], dg_hbm.at[0, pl.ds(at, 256), :], dsem.at[m]).start()
        return carry

    lax.fori_loop(0, feat // 256, down, 0)

    acc[...] = jnp.zeros_like(acc)

    def home(i, carry):
        g = (z + i) % 4
        slab = rec2.at[pl.ds(PL * g, PL)]
        pltpu.make_async_copy(slab, slab, rsem2.at[g]).wait()
        ovf, piece = overflow_rows(rec2, g)
        gm[pl.ds(PL * g, PL), :] = piece(2 * tiles)
        acc[...] += jnp.dot(
            wmain[g], rec2[pl.ds(PL * g, PL), :, 0:feat].reshape(PL * MAIN, feat), preferred_element_type=F32
        ) + jnp.dot(wovf[g], jnp.concatenate(ovf, axis=0).astype(BF16), preferred_element_type=F32)
        return carry

    lax.fori_loop(0, 4, home, 0)
    ig_ref[...] = acc[...].astype(BF16)

    gates = jnp.zeros((128, 128), F32)
    table = gm[...].astype(BF16)
    for k in range(ids_ref.shape[1]):
        hit = ids_ref[:, k : k + 1] == lane
        slot = jnp.sum(jnp.where(hit, sref[...], 0.0), axis=1, keepdims=True)
        line = jnp.dot(hit.astype(BF16)[:, 0:E], table, preferred_element_type=F32)
        value = jnp.sum(jnp.where(lane.astype(F32) == slot, line, 0.0), axis=1, keepdims=True)
        value = value / prob_ref[:, k : k + 1].astype(BF16).astype(F32)
        gates = jnp.where(lane == k, value, gates)
    gg_ref[...] = gates[:, 0 : ids_ref.shape[1]].astype(BF16)

    most = msg.at[pl.ds(0, E - 1)]
    pltpu.make_async_copy(most, most, ssem.at[0]).wait()
    for q in range(2):
        partial_copy(q).wait_send()
        for h in range(2):
            local = jnp.logical_and(z == 2 * f + q, f == h)

            @pl.when(local)
            def _():
                part = msg2.at[q, h, pl.ds(0, PL - 1)]
                pltpu.make_async_copy(part, part, ssem2.at[q, h]).wait()

            @pl.when(jnp.logical_not(local))
            def _():
                pltpu.make_async_copy(msg2.at[q, h], msg2.at[q, h], ssem2.at[q, h]).wait()

    def flush(m, carry):
        at = pl.multiple_of(m * 256, 256)
        pltpu.make_async_copy(dgv.at[m], dg_hbm.at[0, pl.ds(at, 256), :], dsem.at[m]).wait()
        return carry

    lax.fori_loop(0, feat // 256, flush, 0)


def body(out_grad, expert_ids, gate_probs, saved_inputs, gate_weight, up_weight, down_weight):
    tokens, feat = out_grad.shape
    top = expert_ids.shape[1]
    hidden = down_weight.shape[2]
    wide = feat + 256
    dma = pltpu.SemaphoreType.DMA
    vmem = pl.BlockSpec(memory_space=pltpu.VMEM)
    hbm = pl.BlockSpec(memory_space=pl.ANY)
    return pl.pallas_call(
        kernel,
        out_shape=(
            jax.ShapeDtypeStruct((tokens, feat), BF16),
            jax.ShapeDtypeStruct((tokens, top), BF16),
            jax.ShapeDtypeStruct((1, feat, hidden), F32),
        ),
        in_specs=[vmem, vmem, vmem, hbm, hbm, hbm, hbm],
        out_specs=(vmem, vmem, hbm),
        scratch_shapes=[
            pltpu.VMEM((E, MAIN, wide), BF16),
            pltpu.VMEM((E, MAIN, wide), BF16),
            pltpu.VMEM((4, G, feat), BF16),
            pltpu.VMEM((E * 32, 128), F32),
            pltpu.VMEM((2 * G, 2 * feat), BF16),
            pltpu.VMEM((2, G, 2 * feat), BF16),
            pltpu.VMEM((2, feat, hidden), BF16),
            pltpu.VMEM((2, feat, hidden), BF16),
            pltpu.VMEM((feat, hidden), BF16),
            pltpu.VMEM((2, G, hidden), F32),
            pltpu.VMEM((2, G, hidden), F32),
            pltpu.VMEM((2, 2, G, hidden), BF16),
            pltpu.VMEM((2, G, hidden), F32),
            pltpu.VMEM((2, G, hidden), F32),
            pltpu.VMEM((2, G, hidden), F32),
            pltpu.VMEM((G, hidden), BF16),
            pltpu.VMEM((G, hidden), BF16),
            pltpu.VMEM((2, 2, PL, MAIN, wide), BF16),
            pltpu.VMEM((E, MAIN, wide), BF16),
            pltpu.VMEM((4, tokens, PL * MAIN), BF16),
            pltpu.VMEM((4, tokens, G - PL * MAIN), BF16),
            pltpu.VMEM((E, 128), F32),
            pltpu.VMEM((tokens, feat), F32),
            pltpu.VMEM((feat // 256, 256, hidden), F32),
            pltpu.VMEM((tokens, 128), F32),
            pltpu.VMEM((128, tokens), F32),
            pltpu.VMEM((128, tokens), F32),
            dma((4,)),
            dma((2, 2)),
            dma((2,)),
            dma((2, 2)),
            dma((1,)),
            dma((4,)),
            dma((2, 2)),
            dma((4,)),
            dma((feat // 256,)),
        ],
        compiler_params=pltpu.CompilerParams(
            collective_id=0, has_side_effects=True, vmem_limit_bytes=62 << 20
        ),
    )(expert_ids, gate_probs, out_grad, saved_inputs, gate_weight, up_weight, down_weight)


def solution(mesh):
    placed = (
        P("expert", "fsdp"),
        P("expert", None),
        P("expert", None),
        P("expert", "fsdp", None),
        P("expert", "fsdp", None),
        P("expert", "fsdp", None),
        P("expert", "fsdp", None),
    )
    return jax.shard_map(
        body,
        mesh=mesh,
        in_specs=placed,
        out_specs=(P("expert", "fsdp"), P("expert", None), P("expert", "fsdp", None)),
        check_vma=False,
    )
```

time: 232 us -> 108 us (0.47); the launches traced: 228 us -> 108 us
  Pallas kernels: 0 us -> 97.2 us
  blocking collectives: 65.9 us -> 0 us
  waiting for transfers between devices: 56.5 us -> 0 us
  matrix products: 40.2 us -> 0 us
  starting transfers between devices: 21.9 us -> 0 us
  local copies, waits for them, and re-layouts: 26.4 us -> 10.3 us
  between operations: 14 us -> 0.64 us
  other arithmetic: 3.44 us -> 0 us
    pallas_call x0 -> x1, Pallas kernels: none -> 97.2 us  [body(): pl.pallas_call(kernel, out_shape=(jax.ShapeDtypeStruct((tokens, feat), BF...]
    all_to_all x2 -> x0, blocking collectives: 65.9 us -> none  [the longest x1 60.4 us: body(): lax.all_to_all(send_rows, 'expert', split_axis=0, concat_axis=0, tiled=True)]
    dot_general x10 -> x0, matrix products: 40.2 us -> none  [the longest x1 6.92 us: body(): up_pre = jnp.dot(inputs, up_full, preferred_element_type=jnp.float32)]
    all_to_all x4 -> x0, waiting for transfers between devices: 39.2 us -> none  [the longest x1 23.3 us: body(): lax.all_to_all(back_feat, 'expert', split_axis=0, concat_axis=0, tiled=True)]
    all_to_all x8 -> x0, local copies, waits for them, and re-layouts: 22.8 us -> none  [the longest x2 11 us: body(): lax.all_to_all(send_rows, 'expert', split_axis=0, concat_axis=0, tiled=True)]
    all_to_all x4 -> x0, starting transfers between devices: 21.6 us -> none  [the longest x1 7.03 us: body(): lax.all_to_all(send_prob, 'expert', split_axis=0, concat_axis=0, tiled=True)]
    all_gather x3 -> x0, waiting for transfers between devices: 15.6 us -> none  [the longest x1 15.6 us: body(): lax.all_gather(hidden, 'fsdp', axis=0, tiled=True)]
    unnamed x24 -> x4, local copies, waits for them, and re-layouts: 1.62 us -> 8.85 us
  transfers between devices with their start and end apart: 8 -> 0, of which waited for: 5 -> 0; matrix products, arithmetic and copies ran while one was open for 13% -> 0% of each run, Pallas kernels for 0% -> 0%
where the time goes in v1:
time: 108 us
  Pallas kernels  97.2 us (90%)
  local copies, waits for them, and re-layouts  10.3 us (10%)
    pallas_call x1, Pallas kernels, body(): pl.pallas_call(kernel, out_shape=(jax.ShapeDtypeStruct((tokens, feat), BF...  97.2 us
    unnamed x4, local copies, waits for them, and re-layouts  8.85 us

profile of v1, /device:TPU:1, one launch (start us, length us, event | category | flops | bytes accessed | tf_op | source)
XLA Modules:
  0.0 108.1 jit_solution(15752936791868175905)
XLA Ops:
  0.6 1.4 %copy.10.ids_ref = s32[128,6]{1,0:T(8,128)} copy(s32[128,6]{0,1:T(8,128)} %param.8) | data formatting | bytes 6144 | tf_op args[1]
  2.1 1.4 %copy.11.prob_ref = f32[128,6]{1,0:T(8,128)} copy(f32[128,6]{0,1:T(8,128)} %param.9) | data formatting | bytes 6144 | tf_op args[2]
  3.5 97.2 %shard_map.94 = (bf16[128,1280]{1,0:T(8,128)(2,1)}, bf16[128,6]{1,0:T(8,128)(2,1)}, f32[1,1280,768]{2,1,0:T(8,128)}) custom-call(s32[128,6]{1,0:T(8,128)} %copy.10.ids_ref, f32[128,6]{1,0:T(8,128)} %copy.11.prob_ref, bf16[128,1280]{1,0:T(8,128)(2,1)} %og_ref.1, bf16[1,576,2560]{2,1,0:T(8,128)(2,1)} %sin_hbm.1, bf16[1,1280,768]{2,1,0:T(8,128)(2,1)} %gw_hbm.1, ...), custom_call_target="tpu_custom_call" | custom-call | tf_op jit(solution)/shard_map/pallas_call | solution.py:351
  100.7 1.4 %copy.12 = bf16[128,6]{0,1:T(8,128)(2,1)} copy(bf16[128,6]{1,0:T(8,128)(2,1)} %get-tuple-element.4) | data formatting | bytes 3072 | tf_op jit(solution)/shard_map/pallas_call | solution.py:351
  102.1 1.7 %copy.15 = bf16[128,1280]{1,0:T(8,128)(2,1)} copy(bf16[128,1280]{1,0:T(8,128)(2,1)} %get-tuple-element.9) | data formatting | bytes 655360
  103.8 4.3 %copy.16 = f32[1,1280,768]{2,1,0:T(8,128)} copy(f32[1,1280,768]{2,1,0:T(8,128)} %get-tuple-element.11) | data formatting | bytes 7864320

commit v2 on v1

v2 whole, which is shorter than its diff:
```python
import functools

import jax
import jax.numpy as jnp
from jax import lax
from jax.experimental import pallas as pl
from jax.experimental.pallas import tpu as pltpu
from jax.sharding import PartitionSpec as P

MESH = pl.DeviceIdType.MESH
F32 = jnp.float32
BF16 = jnp.bfloat16
E = 64
PL = 16
CAP = 18
MAIN = 16
G = PL * CAP


def iota(shape, dim):
    return lax.broadcasted_iota(jnp.int32, shape, dim)


def target(me, o):
    z, y, x = me // 16, (me // 4) % 4, me % 4
    return ((z + o // 16) % 4) * 16 + ((y + (o // 4) % 4) % 4) * 4 + (x + o % 4) % 4


def near(me, f, dz, yx):
    sign = 1 - 2 * f
    z = (me // 16 + 4 + sign * dz) % 4
    y = ((me // 4) % 4 + 4 + sign * (yx // 4)) % 4
    x = (me % 4 + 4 + sign * (yx % 4)) % 4
    return z * 16 + y * 4 + x


def kernel(
    ids_ref, prob_ref, og_ref, sin_hbm, gw_hbm, uw_hbm, dw_hbm,
    ig_ref, gg_ref, dgv,
    msg, recv, xs, scr, sin, xin, wg, wu, wd, bm, cm, hid, pown, psend, precv, gpg, upg,
    msg2, rec2, wmain, wovf, gm, acc, sref, stref, ptref,
    lsem, wsem, hsem, psem, ssem, rsem, ssem2, rsem2,
):
    me = lax.axis_index("expert")
    f = lax.axis_index("fsdp")
    z = me // PL
    feat = og_ref.shape[1]
    tiles = feat // 128
    top = ids_ref.shape[0]

    loads = [
        pltpu.make_async_copy(sin_hbm.at[0], sin, lsem.at[0]),
        pltpu.make_async_copy(gw_hbm.at[0], wg.at[f], lsem.at[1]),
        pltpu.make_async_copy(uw_hbm.at[0], wu.at[f], lsem.at[2]),
        pltpu.make_async_copy(dw_hbm.at[0], wd, lsem.at[3]),
    ]
    for c in loads:
        c.start()

    barrier = pltpu.get_barrier_semaphore()

    def greet(i, carry):
        d = target(me, i)
        pl.semaphore_signal(barrier, inc=1, device_id=(d, f), device_id_type=MESH)
        pl.semaphore_signal(barrier, inc=1, device_id=(d, 1 - f), device_id_type=MESH)
        return carry

    lax.fori_loop(1, E, greet, 0)
    pl.semaphore_signal(barrier, inc=1, device_id=(me, 1 - f), device_id_type=MESH)

    lane = iota((128, 128), 1)
    row = iota((128, 128), 0)
    names = jnp.zeros((128, 128), F32)
    probs = jnp.zeros((128, 128), F32)
    for k in range(top):
        hit = ids_ref[k : k + 1, :] == row
        names = names + hit.astype(F32)
        probs = probs + jnp.where(hit, prob_ref[k : k + 1, :], 0.0)
    before = (row < lane).astype(BF16)
    rank = jnp.dot(names.astype(BF16), before, preferred_element_type=F32)
    stref[...] = jnp.where(names > 0.0, rank, -1.0)
    ptref[...] = probs

    def place(r):
        main = r < PL * MAIN
        over = r - PL * MAIN
        return jnp.where(main, r // MAIN, over % PL), jnp.where(main, r % MAIN, MAIN + over // PL)

    def pack(ref):
        packed = scr[0 : PL * 32, :].reshape(PL, 32, 128).astype(BF16)
        ref[:, :, feat : feat + 128] = packed[:, 0:16, :]
        ref[:, :, feat + 128 : feat + 256] = packed[:, 16:32, :]

    def build(g):
        who, slot = place(iota((G, 128), 0))
        spread = (who + PL * g == iota((G, 128), 1)).astype(BF16)
        s_rep = jnp.dot(spread, stref[...].astype(BF16), preferred_element_type=F32)
        p_rep = jnp.dot(spread, ptref[...].astype(BF16), preferred_element_type=F32)
        lhs = jnp.where(s_rep == slot.astype(F32), p_rep, 0.0).astype(BF16)
        out = msg.at[pl.ds(PL * g, PL)]
        for n in range(0, feat, 256):
            rows = jnp.dot(lhs, og_ref[:, n : n + 256], preferred_element_type=F32)
            out[:, :, n : n + 256] = rows[0 : PL * MAIN].astype(BF16).reshape(PL, MAIN, 256)
            for c in range(CAP - MAIN):
                for j in range(2):
                    scr[pl.ds(c * tiles + n // 128 + j, PL, stride=32), :] = rows[
                        PL * (MAIN + c) : PL * (MAIN + c + 1), 128 * j : 128 * (j + 1)
                    ]
        pack(out)

    def dispatch(phase):
        def step(i, carry):
            d = near(me, f, 1 - phase + 2 * (i % 2), ((i // 2) * 7) % PL)
            pltpu.make_async_remote_copy(
                src_ref=msg.at[d], dst_ref=recv.at[me], send_sem=ssem.at[0], recv_sem=rsem.at[z],
                device_id=(d, f), device_id_type=MESH,
            ).start()
            return carry

        lax.fori_loop(phase, 32, step, 0)

    def weight_copies():
        return [
            pltpu.make_async_remote_copy(
                src_ref=h.at[0], dst_ref=w.at[f], send_sem=wsem.at[0, i], recv_sem=wsem.at[1, i],
                device_id=(me, 1 - f), device_id_type=MESH,
            )
            for i, (h, w) in enumerate(((gw_hbm, wg), (uw_hbm, wu)))
        ]

    scr[...] = jnp.zeros_like(scr)

    def build_odd(i, carry):
        build((z + 1 + 2 * i) % 4)
        return carry

    lax.fori_loop(0, 2, build_odd, 0)
    pl.semaphore_wait(barrier, 2 * (E - 1) + 1)
    dispatch(0)
    for c in weight_copies():
        c.start()

    def build_even(i, carry):
        build((z + 2 * i) % 4)
        return carry

    lax.fori_loop(0, 2, build_even, 0)
    dispatch(1)
    pltpu.make_async_copy(msg.at[me], recv.at[me], rsem.at[z]).start()

    sref[...] = stref[...].T
    s_half = sref[...].astype(BF16)
    for g in range(4):
        who, slot = place(iota((128, G), 1))
        spread = (who + PL * g == iota((128, G), 0)).astype(BF16)
        s_rep = jnp.dot(s_half, spread, preferred_element_type=F32)
        hot = (s_rep == slot.astype(F32)).astype(BF16)
        wmain[g] = hot[:, 0 : PL * MAIN]
        wovf[g] = hot[:, PL * MAIN : G]

    loads[0].wait()
    who, slot = place(iota((G, G), 0))
    perm = (CAP * who + slot == iota((G, G), 1)).astype(BF16)
    for q in range(2):
        for n in range(0, 2 * feat, 512):
            xin[q, :, n : n + 512] = jnp.dot(
                perm, sin[G * q : G * (q + 1), n : n + 512], preferred_element_type=F32
            ).astype(BF16)

    loads[1].wait()
    loads[2].wait()
    for c in weight_copies():
        c.wait()
    for n in range(0, wd.shape[1], 256):
        cols = slice(n, n + 256)

        def gated(q, carry):
            a, b = xin[q, :, 0:feat], xin[q, :, feat : 2 * feat]
            gate = jnp.dot(a, wg[0, :, cols], preferred_element_type=F32) + jnp.dot(
                b, wg[1, :, cols], preferred_element_type=F32
            )
            up = jnp.dot(a, wu[0, :, cols], preferred_element_type=F32) + jnp.dot(
                b, wu[1, :, cols], preferred_element_type=F32
            )
            sg = jax.nn.sigmoid(gate)
            silu = gate * sg
            cm[q, :, cols] = silu
            bm[q, :, cols] = up * sg * (1.0 + gate * (1.0 - sg))
            hid[f, q, :, cols] = (silu * up).astype(BF16)
            return carry

        lax.fori_loop(0, 2, gated, 0)

    hid_copy = pltpu.make_async_remote_copy(
        src_ref=hid.at[f], dst_ref=hid.at[f], send_sem=hsem.at[0], recv_sem=hsem.at[1],
        device_id=(me, 1 - f), device_id_type=MESH,
    )
    hid_copy.start()
    loads[3].wait()

    def overflow_rows(ref, g):
        tail = ref[pl.ds(PL * g, PL), :, feat : feat + 256].astype(F32)
        for h in range(2):
            scr[pl.ds(PL * MAIN * h, PL * MAIN), :] = tail[:, :, 128 * h : 128 * (h + 1)].reshape(
                PL * MAIN, 128
            )

        def piece(i):
            return scr[pl.ds(PL * MAIN * (i // MAIN) + i % MAIN, PL, stride=MAIN), :]

        return [
            jnp.concatenate([piece(c * tiles + j) for j in range(tiles)], axis=1) for c in range(CAP - MAIN)
        ], piece

    def unpack(g):
        slab = recv.at[pl.ds(PL * g, PL)]
        pltpu.make_async_copy(slab, slab, rsem.at[g]).wait()
        xs[g, 0 : PL * MAIN, :] = recv[pl.ds(PL * g, PL), :, 0:feat].reshape(PL * MAIN, feat)
        ovf, _ = overflow_rows(recv, g)
        xs[g, PL * MAIN : G, :] = jnp.concatenate(ovf, axis=0).astype(BF16)

    def partial_copy(q):
        return pltpu.make_async_remote_copy(
            src_ref=psend.at[q], dst_ref=precv.at[q], send_sem=psem.at[0, q], recv_sem=psem.at[1, q],
            device_id=(me, 1 - f), device_id_type=MESH,
        )

    def back(i, carry):
        q = (z + 1 + i) % 2
        unpack(2 * (1 - f) + q)
        psend[q] = jnp.dot(xs[2 * (1 - f) + q], wd[...], preferred_element_type=F32)
        partial_copy(q).start()
        unpack(2 * f + q)
        pown[...] = jnp.dot(xs[2 * f + q], wd[...], preferred_element_type=F32)
        partial_copy(q).wait_recv()
        raw = pown[...] + precv[q]
        gpg[...] = (raw * bm[q]).astype(BF16)
        upg[...] = (raw * cm[q]).astype(BF16)
        gates = jnp.sum(raw * hid[f, q].astype(F32), axis=1, keepdims=True)
        r, ln = iota((PL * MAIN, 128), 0), iota((PL * MAIN, 128), 1)
        table = jnp.where(ln == r % MAIN, gates[0 : PL * MAIN], 0.0).reshape(PL, MAIN, 128).sum(axis=1)
        r, ln = iota((G - PL * MAIN, 128), 0), iota((G - PL * MAIN, 128), 1)
        table = table + jnp.where(ln == MAIN + r // PL, gates[PL * MAIN : G], 0.0).reshape(
            CAP - MAIN, PL, 128
        ).sum(axis=0)
        for h in range(2):
            out = msg2.at[q, h]
            for n in range(0, feat, 256):
                rows = lax.dot_general(
                    gpg[...], wg[h, n : n + 256, :], (((1,), (1,)), ((), ())), preferred_element_type=F32
                ) + lax.dot_general(
                    upg[...], wu[h, n : n + 256, :], (((1,), (1,)), ((), ())), preferred_element_type=F32
                )
                out[:, :, n : n + 256] = rows[0 : PL * MAIN].astype(BF16).reshape(PL, MAIN, 256)
                for c in range(CAP - MAIN):
                    for jj in range(2):
                        scr[pl.ds(c * tiles + n // 128 + jj, PL, stride=32), :] = rows[
                            PL * (MAIN + c) : PL * (MAIN + c + 1), 128 * jj : 128 * (jj + 1)
                        ]
            scr[pl.ds(2 * tiles, PL, stride=32), :] = table
            pack(out)

            def send(j, carry):
                blk = near((2 * f + q) * PL + me % PL, f, 0, (j * 7) % PL)
                here = jnp.logical_and(blk == me, h == f)

                @pl.when(here)
                def _():
                    pltpu.make_async_copy(out.at[blk % PL], rec2.at[me], rsem2.at[z]).start()

                @pl.when(jnp.logical_not(here))
                def _():
                    pltpu.make_async_remote_copy(
                        src_ref=out.at[blk % PL], dst_ref=rec2.at[me], send_sem=ssem2.at[q, h],
                        recv_sem=rsem2.at[z], device_id=(blk, h), device_id_type=MESH,
                    ).start()

                return carry

            lax.fori_loop(0, PL, send, 0)
        return carry

    lax.fori_loop(0, 2, back, 0)

    hid_copy.wait()
    inner = hid.shape[3]

    def down(m, carry):
        at = pl.multiple_of(m * 256, 256)
        lhs = xs[:, :, pl.ds(at, 256)].reshape(4 * G, 256)
        dgv[0, pl.ds(at, 256), :] = lax.dot_general(
            lhs, hid[...].reshape(4 * G, inner), (((0,), (0,)), ((), ())), preferred_element_type=F32
        )
        return carry

    lax.fori_loop(0, feat // 256, down, 0)

    acc[...] = jnp.zeros_like(acc)

    def home(i, carry):
        g = (z + 1 + 2 * i - 3 * (i // 2)) % 4
        slab = rec2.at[pl.ds(PL * g, PL)]
        pltpu.make_async_copy(slab, slab, rsem2.at[g]).wait()
        ovf, piece = overflow_rows(rec2, g)
        gm[pl.ds(PL * g, PL), :] = piece(2 * tiles)
        acc[...] += jnp.dot(
            wmain[g], rec2[pl.ds(PL * g, PL), :, 0:feat].reshape(PL * MAIN, feat), preferred_element_type=F32
        ) + jnp.dot(wovf[g], jnp.concatenate(ovf, axis=0).astype(BF16), preferred_element_type=F32)
        return carry

    lax.fori_loop(0, 4, home, 0)
    ig_ref[...] = acc[...].astype(BF16)

    table = gm[...].astype(BF16)
    values = jnp.zeros((8, 128), F32)
    for k in range(top):
        hit = ids_ref[k : k + 1, :] == row
        slot = jnp.sum(jnp.where(hit, stref[...], 0.0), axis=0, keepdims=True)
        line = lax.dot_general(
            table, hit.astype(BF16)[0:E, :], (((0,), (0,)), ((), ())), preferred_element_type=F32
        )
        value = jnp.sum(jnp.where(row.astype(F32) == slot, line, 0.0), axis=0, keepdims=True)
        value = value / prob_ref[k : k + 1, :].astype(BF16).astype(F32)
        values = jnp.where(row[0:8] == k, value, values)
    gg_ref[...] = values[0:top].astype(BF16)

    most = msg.at[pl.ds(0, E - 1)]
    pltpu.make_async_copy(most, most, ssem.at[0]).wait()
    for q in range(2):
        partial_copy(q).wait_send()
        for h in range(2):
            local = jnp.logical_and(z == 2 * f + q, f == h)

            @pl.when(local)
            def _():
                part = msg2.at[q, h, pl.ds(0, PL - 1)]
                pltpu.make_async_copy(part, part, ssem2.at[q, h]).wait()

            @pl.when(jnp.logical_not(local))
            def _():
                pltpu.make_async_copy(msg2.at[q, h], msg2.at[q, h], ssem2.at[q, h]).wait()


def body(out_grad, expert_ids, gate_probs, saved_inputs, gate_weight, up_weight, down_weight):
    tokens, feat = out_grad.shape
    top = expert_ids.shape[1]
    hidden = down_weight.shape[2]
    wide = feat + 256
    dma = pltpu.SemaphoreType.DMA
    vmem = pl.BlockSpec(memory_space=pltpu.VMEM)
    hbm = pl.BlockSpec(memory_space=pl.ANY)
    input_grad, gate_grad, down_grad = pl.pallas_call(
        kernel,
        out_shape=(
            pltpu.VMEM((tokens, feat), BF16),
            pltpu.VMEM((top, tokens), BF16),
            pltpu.VMEM((1, feat, hidden), F32),
        ),
        in_specs=[vmem, vmem, vmem, hbm, hbm, hbm, hbm],
        out_specs=(vmem, vmem, vmem),
        scratch_shapes=[
            pltpu.VMEM((E, MAIN, wide), BF16),
            pltpu.VMEM((E, MAIN, wide), BF16),
            pltpu.VMEM((4, G, feat), BF16),
            pltpu.VMEM((E * 32, 128), F32),
            pltpu.VMEM((2 * G, 2 * feat), BF16),
            pltpu.VMEM((2, G, 2 * feat), BF16),
            pltpu.VMEM((2, feat, hidden), BF16),
            pltpu.VMEM((2, feat, hidden), BF16),
            pltpu.VMEM((feat, hidden), BF16),
            pltpu.VMEM((2, G, hidden), F32),
            pltpu.VMEM((2, G, hidden), F32),
            pltpu.VMEM((2, 2, G, hidden), BF16),
            pltpu.VMEM((G, hidden), F32),
            pltpu.VMEM((2, G, hidden), F32),
            pltpu.VMEM((2, G, hidden), F32),
            pltpu.VMEM((G, hidden), BF16),
            pltpu.VMEM((G, hidden), BF16),
            pltpu.VMEM((2, 2, PL, MAIN, wide), BF16),
            pltpu.VMEM((E, MAIN, wide), BF16),
            pltpu.VMEM((4, tokens, PL * MAIN), BF16),
            pltpu.VMEM((4, tokens, G - PL * MAIN), BF16),
            pltpu.VMEM((E, 128), F32),
            pltpu.VMEM((tokens, feat), F32),
            pltpu.VMEM((tokens, 128), F32),
            pltpu.VMEM((128, tokens), F32),
            pltpu.VMEM((128, tokens), F32),
            dma((4,)),
            dma((2, 2)),
            dma((2,)),
            dma((2, 2)),
            dma((1,)),
            dma((4,)),
            dma((2, 2)),
            dma((4,)),
        ],
        compiler_params=pltpu.CompilerParams(
            collective_id=0, has_side_effects=True, vmem_limit_bytes=50 << 20
        ),
    )(expert_ids.T, gate_probs.T, out_grad, saved_inputs, gate_weight, up_weight, down_weight)
    return input_grad, gate_grad.T, down_grad


def solution(mesh):
    placed = (
        P("expert", "fsdp"),
        P("expert", None),
        P("expert", None),
        P("expert", "fsdp", None),
        P("expert", "fsdp", None),
        P("expert", "fsdp", None),
        P("expert", "fsdp", None),
    )
    return jax.shard_map(
        body,
        mesh=mesh,
        in_specs=placed,
        out_specs=(P("expert", "fsdp"), P("expert", None), P("expert", "fsdp", None)),
        check_vma=False,
    )
```

time: 108 us -> 90 us (0.83)
  Pallas kernels: 97.2 us -> 86 us
  local copies, waits for them, and re-layouts: 10.3 us -> 3.23 us
    pallas_call x1, Pallas kernels: 97.2 us -> 86 us  [body(): pl.pallas_call(kernel, out_shape=(pltpu.VMEM((tokens, feat), BF16), pltpu...]
    unnamed x4 -> x3, local copies, waits for them, and re-layouts: 8.85 us -> 3.23 us
    pallas_call x1 -> x0, local copies, waits for them, and re-layouts: 1.42 us -> none  [body(): pl.pallas_call(kernel, out_shape=(jax.ShapeDtypeStruct((tokens, feat), BF...]
where the time goes in v2:
time: 90 us; the launch traced here: 89.9 us
  Pallas kernels  86 us (96%)
  local copies, waits for them, and re-layouts  3.23 us (4%)
    pallas_call x1, Pallas kernels, body(): pl.pallas_call(kernel, out_shape=(pltpu.VMEM((tokens, feat), BF16), pltpu...  86 us
    unnamed x3, local copies, waits for them, and re-layouts  3.23 us

profile of v2, /device:TPU:1, one launch (start us, length us, event | category | flops | bytes accessed | tf_op | source)
XLA Modules:
  0.0 89.9 jit_solution(7286073894064682450)
XLA Ops:
  0.6 86.0 %shard_map.94 = (bf16[128,1280]{1,0:T(8,128)(2,1)S(1)}, bf16[6,128]{1,0:T(8,128)(2,1)S(1)}, f32[1,1280,768]{2,1,0:T(8,128)S(1)}) custom-call(s32[6,128]{1,0:T(8,128)} %bitcast.4, f32[6,128]{1,0:T(8,128)} %bitcast.5, bf16[128,1280]{1,0:T(8,128)(2,1)} %og_ref.1, bf16[1,576,2560]{2,1,0:T(8,128)(2,1)} %sin_hbm.1, bf16[1,1280,768]{2,1,0:T(8,128)(2,1)} %gw_hbm.1, ...), custom_call_target="tpu_custom_call" | custom-call | tf_op jit(solution)/shard_map/pallas_call | solution.py:352
  86.6 0.7 copy.13
  87.4 0.6 copy.14
  88.0 1.9 %copy.15 = f32[1,1280,768]{2,1,0:T(8,128)} copy(f32[1,1280,768]{2,1,0:T(8,128)S(1)} %get-tuple-element.11) | data formatting | bytes 7864320

commit v3 on v2

v3 whole, which is shorter than its diff:
```python
import functools

import jax
import jax.numpy as jnp
from jax import lax
from jax.experimental import pallas as pl
from jax.experimental.pallas import tpu as pltpu
from jax.sharding import PartitionSpec as P

MESH = pl.DeviceIdType.MESH
F32 = jnp.float32
BF16 = jnp.bfloat16
E = 64
PL = 16
CAP = 18
MAIN = 16
REST = CAP - MAIN
G = PL * CAP


def iota(shape, dim):
    return lax.broadcasted_iota(jnp.int32, shape, dim)


def near(me, f, dz, yx):
    sign = 1 - 2 * f
    z = (me // 16 + 4 + sign * dz) % 4
    y = ((me // 4) % 4 + 4 + sign * (yx // 4)) % 4
    x = (me % 4 + 4 + sign * (yx % 4)) % 4
    return z * 16 + y * 4 + x


def kernel(
    ids_ref, prob_ref, og_ref, sin_hbm, gw_hbm, uw_hbm, dw_hbm,
    ig_ref, gg_ref, dgv,
    msg, over, recv, recvo, xs, sin, xin, wg, wu, wd, bm, cm, hid, pown, psend, precv, gpg, upg,
    msg2, over2, rec2, rec2o, wmain, wovf, gm, acc, sref, stref, ptref,
    lsem, wsem, hsem, psem, ssem, rsem, ssem2, rsem2, met,
):
    me = lax.axis_index("expert")
    f = lax.axis_index("fsdp")
    z = me // PL
    feat = og_ref.shape[1]
    top = ids_ref.shape[0]

    loads = [
        pltpu.make_async_copy(sin_hbm.at[0], sin, lsem.at[0]),
        pltpu.make_async_copy(gw_hbm.at[0], wg.at[f], lsem.at[1]),
        pltpu.make_async_copy(uw_hbm.at[0], wu.at[f], lsem.at[2]),
        pltpu.make_async_copy(dw_hbm.at[0], wd, lsem.at[3]),
    ]
    for c in loads:
        c.start()

    barrier = pltpu.get_barrier_semaphore()

    def greet(i, carry):
        d = near(me, f, 1 + 2 * (i % 2), i // 2)
        pl.semaphore_signal(barrier, inc=1, device_id=(d, f), device_id_type=MESH)
        return carry

    lax.fori_loop(0, 32, greet, 0)
    pl.semaphore_signal(barrier, inc=1, device_id=(me, 1 - f), device_id_type=MESH)

    lane = iota((128, 128), 1)
    row = iota((128, 128), 0)
    names = jnp.zeros((128, 128), F32)
    probs = jnp.zeros((128, 128), F32)
    for k in range(top):
        hit = ids_ref[k : k + 1, :] == row
        names = names + hit.astype(F32)
        probs = probs + jnp.where(hit, prob_ref[k : k + 1, :], 0.0)
    before = (row < lane).astype(BF16)
    rank = jnp.dot(names.astype(BF16), before, preferred_element_type=F32)
    stref[...] = jnp.where(names > 0.0, rank, -1.0)
    ptref[...] = probs

    def place(r):
        main = r < PL * MAIN
        rest = r - PL * MAIN
        return jnp.where(main, r // MAIN, rest // REST), jnp.where(main, r % MAIN, MAIN + rest % REST)

    def build(g):
        who, slot = place(iota((G, 128), 0))
        spread = (who + PL * g == iota((G, 128), 1)).astype(BF16)
        s_rep = jnp.dot(spread, stref[...].astype(BF16), preferred_element_type=F32)
        p_rep = jnp.dot(spread, ptref[...].astype(BF16), preferred_element_type=F32)
        lhs = jnp.where(s_rep == slot.astype(F32), p_rep, 0.0).astype(BF16)
        for n in range(0, feat, 256):
            rows = jnp.dot(lhs, og_ref[:, n : n + 256], preferred_element_type=F32).astype(BF16)
            msg[pl.ds(PL * g, PL), :, n : n + 256] = rows[0 : PL * MAIN].reshape(PL, MAIN, 256)
            over[pl.ds(PL * g, PL), :, n : n + 256] = rows[PL * MAIN : G].reshape(PL, REST, 256)

    def dispatch(phase):
        def step(i, carry):
            j = (i * 5) % 32
            d = near(me, f, 1 - phase + 2 * (j // PL), j % PL)
            for b, (src, dst) in enumerate(((msg, recv), (over, recvo))):
                pltpu.make_async_remote_copy(
                    src_ref=src.at[d], dst_ref=dst.at[me], send_sem=ssem.at[b], recv_sem=rsem.at[b, z],
                    device_id=(d, f), device_id_type=MESH,
                ).start()
            return carry

        lax.fori_loop(phase, 32, step, 0)

    def weight_copies():
        return [
            pltpu.make_async_remote_copy(
                src_ref=h.at[0], dst_ref=w.at[f], send_sem=wsem.at[0, i], recv_sem=wsem.at[1, i],
                device_id=(me, 1 - f), device_id_type=MESH,
            )
            for i, (h, w) in enumerate(((gw_hbm, wg), (uw_hbm, wu)))
        ]

    def build_odd(i, carry):
        build((z + 1 + 2 * i) % 4)
        return carry

    lax.fori_loop(0, 2, build_odd, 0)
    pl.semaphore_wait(barrier, 33)
    pl.semaphore_signal(met.at[0], inc=1, device_id=((me + PL) % E, f), device_id_type=MESH)
    dispatch(0)
    for c in weight_copies():
        c.start()

    def build_even(i, carry):
        build((z + 2 * i) % 4)
        return carry

    lax.fori_loop(0, 2, build_even, 0)
    pl.semaphore_wait(met.at[0], 1)
    pl.semaphore_signal(met.at[1], inc=1, device_id=(me, 1 - f), device_id_type=MESH)
    dispatch(1)
    pltpu.make_async_copy(msg.at[me], recv.at[me], rsem.at[0, z]).start()
    pltpu.make_async_copy(over.at[me], recvo.at[me], rsem.at[1, z]).start()

    sref[...] = stref[...].T
    s_half = sref[...].astype(BF16)
    for g in range(4):
        who, slot = place(iota((128, G), 1))
        spread = (who + PL * g == iota((128, G), 0)).astype(BF16)
        s_rep = jnp.dot(s_half, spread, preferred_element_type=F32)
        hot = (s_rep == slot.astype(F32)).astype(BF16)
        wmain[g] = hot[:, 0 : PL * MAIN]
        wovf[g] = hot[:, PL * MAIN : G]

    loads[0].wait()
    who, slot = place(iota((G, G), 0))
    perm = (CAP * who + slot == iota((G, G), 1)).astype(BF16)
    for q in range(2):
        for n in range(0, 2 * feat, 512):
            xin[q, :, n : n + 512] = jnp.dot(
                perm, sin[G * q : G * (q + 1), n : n + 512], preferred_element_type=F32
            ).astype(BF16)

    loads[1].wait()
    loads[2].wait()
    for c in weight_copies():
        c.wait()
    for n in range(0, wd.shape[1], 256):
        cols = slice(n, n + 256)

        def gated(q, carry):
            a, b = xin[q, :, 0:feat], xin[q, :, feat : 2 * feat]
            gate = jnp.dot(a, wg[0, :, cols], preferred_element_type=F32) + jnp.dot(
                b, wg[1, :, cols], preferred_element_type=F32
            )
            up = jnp.dot(a, wu[0, :, cols], preferred_element_type=F32) + jnp.dot(
                b, wu[1, :, cols], preferred_element_type=F32
            )
            sg = jax.nn.sigmoid(gate)
            silu = gate * sg
            cm[q, :, cols] = silu
            bm[q, :, cols] = up * sg * (1.0 + gate * (1.0 - sg))
            hid[f, q, :, cols] = (silu * up).astype(BF16)
            return carry

        lax.fori_loop(0, 2, gated, 0)

    hid_copy = pltpu.make_async_remote_copy(
        src_ref=hid.at[f], dst_ref=hid.at[f], send_sem=hsem.at[0], recv_sem=hsem.at[1],
        device_id=(me, 1 - f), device_id_type=MESH,
    )
    hid_copy.start()
    loads[3].wait()

    def arrived(refs, sems, g):
        for b, ref in enumerate(refs):
            slab = ref.at[pl.ds(PL * g, PL)]
            pltpu.make_async_copy(slab, slab, sems.at[b, g]).wait()

    def unpack(g):
        arrived((recv, recvo), rsem, g)
        xs[g, 0 : PL * MAIN, :] = recv[pl.ds(PL * g, PL)].reshape(PL * MAIN, feat)
        xs[g, PL * MAIN : G, :] = recvo[pl.ds(PL * g, PL)].reshape(PL * REST, feat)

    def partial_copy(q):
        return pltpu.make_async_remote_copy(
            src_ref=psend.at[q], dst_ref=precv.at[q], send_sem=psem.at[0, q], recv_sem=psem.at[1, q],
            device_id=(me, 1 - f), device_id_type=MESH,
        )

    def back(i, carry):
        q = (z + 1 + i) % 2
        unpack(2 * (1 - f) + q)
        psend[q] = jnp.dot(xs[2 * (1 - f) + q], wd[...], preferred_element_type=F32)
        partial_copy(q).start()
        unpack(2 * f + q)
        pown[...] = jnp.dot(xs[2 * f + q], wd[...], preferred_element_type=F32)
        partial_copy(q).wait_recv()
        raw = pown[...] + precv[q]
        gpg[...] = (raw * bm[q]).astype(BF16)
        upg[...] = (raw * cm[q]).astype(BF16)
        gates = jnp.sum(raw * hid[f, q].astype(F32), axis=1, keepdims=True)
        _, slot = place(iota((G, 128), 0))
        spread = jnp.where(iota((G, 128), 1) == slot, gates, 0.0).astype(BF16)
        who, _ = place(iota((PL * REST, G), 1))
        table = jnp.dot(
            (who == iota((PL * REST, G), 0) // REST).astype(BF16), spread, preferred_element_type=F32
        ).astype(BF16)
        for h in range(2):
            over2[q, h, :, :, feat : feat + 128] = table.reshape(PL, REST, 128)
            for n in range(0, feat, 256):
                rows = (
                    lax.dot_general(
                        gpg[...], wg[h, n : n + 256, :], (((1,), (1,)), ((), ())), preferred_element_type=F32
                    )
                    + lax.dot_general(
                        upg[...], wu[h, n : n + 256, :], (((1,), (1,)), ((), ())), preferred_element_type=F32
                    )
                ).astype(BF16)
                msg2[q, h, :, :, n : n + 256] = rows[0 : PL * MAIN].reshape(PL, MAIN, 256)
                over2[q, h, :, :, n : n + 256] = rows[PL * MAIN : G].reshape(PL, REST, 256)

            def send(j, carry):
                blk = near((2 * f + q) * PL + me % PL, f, 0, (j * 5) % PL)
                here = jnp.logical_and(blk == me, h == f)

                for b, (src, dst) in enumerate(((msg2, rec2), (over2, rec2o))):

                    @pl.when(here)
                    def _():
                        pltpu.make_async_copy(src.at[q, h, blk % PL], dst.at[me], rsem2.at[b, z]).start()

                    @pl.when(jnp.logical_not(here))
                    def _():
                        pltpu.make_async_remote_copy(
                            src_ref=src.at[q, h, blk % PL], dst_ref=dst.at[me], send_sem=ssem2.at[b, q, h],
                            recv_sem=rsem2.at[b, z], device_id=(blk, h), device_id_type=MESH,
                        ).start()

                return carry

            lax.fori_loop(0, PL, send, 0)
        return carry

    pl.semaphore_wait(met.at[1], 1)
    lax.fori_loop(0, 2, back, 0)

    hid_copy.wait()
    inner = hid.shape[3]

    def down(m, carry):
        at = pl.multiple_of(m * 256, 256)
        lhs = xs[:, :, pl.ds(at, 256)].reshape(4 * G, 256)
        dgv[0, pl.ds(at, 256), :] = lax.dot_general(
            lhs, hid[...].reshape(4 * G, inner), (((0,), (0,)), ((), ())), preferred_element_type=F32
        )
        return carry

    lax.fori_loop(0, feat // 256, down, 0)

    acc[...] = jnp.zeros_like(acc)

    def home(i, carry):
        g = (z + 1 + 2 * i - 3 * (i // 2)) % 4
        arrived((rec2, rec2o), rsem2, g)
        rest = rec2o[pl.ds(PL * g, PL)].reshape(PL * REST, feat + 128)
        gm[g] = rest[:, feat : feat + 128]
        acc[...] += jnp.dot(
            wmain[g], rec2[pl.ds(PL * g, PL)].reshape(PL * MAIN, feat), preferred_element_type=F32
        ) + jnp.dot(wovf[g], rest[:, 0:feat], preferred_element_type=F32)
        return carry

    lax.fori_loop(0, 4, home, 0)
    ig_ref[...] = acc[...].astype(BF16)

    table = gm[...].reshape(E * REST, 128)
    values = jnp.zeros((8, 128), F32)
    for k in range(top):
        hit = ids_ref[k : k + 1, :] == row
        slot = jnp.sum(jnp.where(hit, stref[...], 0.0), axis=0, keepdims=True)
        once = jnp.logical_and(ids_ref[k : k + 1, :] == row // REST, row % REST == 0)
        line = lax.dot_general(
            table, once.astype(BF16), (((0,), (0,)), ((), ())), preferred_element_type=F32
        )
        value = jnp.sum(jnp.where(row.astype(F32) == slot, line, 0.0), axis=0, keepdims=True)
        value = value / prob_ref[k : k + 1, :].astype(BF16).astype(F32)
        values = jnp.where(row[0:8] == k, value, values)
    gg_ref[...] = values[0:top].astype(BF16)

    for b, ref in enumerate((msg, over)):
        most = ref.at[pl.ds(0, E - 1)]
        pltpu.make_async_copy(most, most, ssem.at[b]).wait()
    for q in range(2):
        partial_copy(q).wait_send()
        for h in range(2):
            local = jnp.logical_and(z == 2 * f + q, f == h)

            for b, ref in enumerate((msg2, over2)):

                @pl.when(local)
                def _():
                    part = ref.at[q, h, pl.ds(0, PL - 1)]
                    pltpu.make_async_copy(part, part, ssem2.at[b, q, h]).wait()

                @pl.when(jnp.logical_not(local))
                def _():
                    pltpu.make_async_copy(ref.at[q, h], ref.at[q, h], ssem2.at[b, q, h]).wait()


def flush(ig_ref, gg_ref, dg_ref, ig_out, gg_out, dg_out, sems):
    parts = 4
    rows = dg_ref.shape[1] // parts
    copies = [
        pltpu.make_async_copy(dg_ref.at[0, pl.ds(rows * i, rows)], dg_out.at[0, pl.ds(rows * i, rows)], sems.at[i])
        for i in range(parts)
    ]
    copies.append(pltpu.make_async_copy(ig_ref, ig_out, sems.at[parts]))
    copies.append(pltpu.make_async_copy(gg_ref, gg_out, sems.at[parts + 1]))
    for c in copies:
        c.start()
    for c in copies:
        c.wait()


def body(out_grad, expert_ids, gate_probs, saved_inputs, gate_weight, up_weight, down_weight):
    tokens, feat = out_grad.shape
    top = expert_ids.shape[1]
    hidden = down_weight.shape[2]
    wide = feat + 128
    dma = pltpu.SemaphoreType.DMA
    vmem = pl.BlockSpec(memory_space=pltpu.VMEM)
    hbm = pl.BlockSpec(memory_space=pl.ANY)
    results = pl.pallas_call(
        kernel,
        out_shape=(
            pltpu.VMEM((tokens, feat), BF16),
            pltpu.VMEM((top, tokens), BF16),
            pltpu.VMEM((1, feat, hidden), F32),
        ),
        in_specs=[vmem, vmem, vmem, hbm, hbm, hbm, hbm],
        out_specs=(vmem, vmem, vmem),
        scratch_shapes=[
            pltpu.VMEM((E, MAIN, feat), BF16),
            pltpu.VMEM((E, REST, feat), BF16),
            pltpu.VMEM((E, MAIN, feat), BF16),
            pltpu.VMEM((E, REST, feat), BF16),
            pltpu.VMEM((4, G, feat), BF16),
            pltpu.VMEM((2 * G, 2 * feat), BF16),
            pltpu.VMEM((2, G, 2 * feat), BF16),
            pltpu.VMEM((2, feat, hidden), BF16),
            pltpu.VMEM((2, feat, hidden), BF16),
            pltpu.VMEM((feat, hidden), BF16),
            pltpu.VMEM((2, G, hidden), F32),
            pltpu.VMEM((2, G, hidden), F32),
            pltpu.VMEM((2, 2, G, hidden), BF16),
            pltpu.VMEM((G, hidden), F32),
            pltpu.VMEM((2, G, hidden), F32),
            pltpu.VMEM((2, G, hidden), F32),
            pltpu.VMEM((G, hidden), BF16),
            pltpu.VMEM((G, hidden), BF16),
            pltpu.VMEM((2, 2, PL, MAIN, feat), BF16),
            pltpu.VMEM((2, 2, PL, REST, wide), BF16),
            pltpu.VMEM((E, MAIN, feat), BF16),
            pltpu.VMEM((E, REST, wide), BF16),
            pltpu.VMEM((4, tokens, PL * MAIN), BF16),
            pltpu.VMEM((4, tokens, G - PL * MAIN), BF16),
            pltpu.VMEM((4, PL * REST, 128), BF16),
            pltpu.VMEM((tokens, feat), F32),
            pltpu.VMEM((tokens, 128), F32),
            pltpu.VMEM((128, tokens), F32),
            pltpu.VMEM((128, tokens), F32),
            dma((4,)),
            dma((2, 2)),
            dma((2,)),
            dma((2, 2)),
            dma((2,)),
            dma((2, 4)),
            dma((2, 2, 2)),
            dma((2, 4)),
            pltpu.SemaphoreType.REGULAR((2,)),
        ],
        compiler_params=pltpu.CompilerParams(
            collective_id=0, has_side_effects=True, vmem_limit_bytes=50 << 20
        ),
    )(expert_ids.T, gate_probs.T, out_grad, saved_inputs, gate_weight, up_weight, down_weight)
    input_grad, gate_grad, down_grad = pl.pallas_call(
        flush,
        out_shape=(
            pltpu.HBM((tokens, feat), BF16),
            pltpu.HBM((top, tokens), BF16),
            pltpu.HBM((1, feat, hidden), F32),
        ),
        in_specs=[vmem, vmem, vmem],
        out_specs=(hbm, hbm, hbm),
        scratch_shapes=[dma((6,))],
        compiler_params=pltpu.CompilerParams(vmem_limit_bytes=4 << 20),
    )(*[pltpu.with_memory_space_constraint(r, pltpu.VMEM) for r in results])
    return input_grad, gate_grad.T, down_grad


def solution(mesh):
    placed = (
        P("expert", "fsdp"),
        P("expert", None),
        P("expert", None),
        P("expert", "fsdp", None),
        P("expert", "fsdp", None),
        P("expert", "fsdp", None),
        P("expert", "fsdp", None),
    )
    return jax.shard_map(
        body,
        mesh=mesh,
        in_specs=placed,
        out_specs=(P("expert", "fsdp"), P("expert", None), P("expert", "fsdp", None)),
        check_vma=False,
    )
```

time: 90 us -> 84.5 us (0.939)
  local copies, waits for them, and re-layouts: 3.23 us -> 0 us
  Pallas kernels: 86 us -> 83.7 us
    pallas_call x1, Pallas kernels: 86 us -> 81.6 us  [body(): pl.pallas_call(kernel, out_shape=(pltpu.VMEM((tokens, feat), BF16), pltpu...]
    unnamed x3 -> x0, local copies, waits for them, and re-layouts: 3.23 us -> none
    pallas_call x0 -> x1, Pallas kernels: none -> 2.07 us  [body(): pl.pallas_call(flush, out_shape=(pltpu.HBM((tokens, feat), BF16), pltpu.H...]
where the time goes in v3:
time: 84.5 us; the launch traced here: 84.3 us
  Pallas kernels  83.7 us (99%)
    pallas_call x1, Pallas kernels, body(): pl.pallas_call(kernel, out_shape=(pltpu.VMEM((tokens, feat), BF16), pltpu...  81.6 us
    pallas_call x1, Pallas kernels, body(): pl.pallas_call(flush, out_shape=(pltpu.HBM((tokens, feat), BF16), pltpu.H...  2.07 us

profile of v3, /device:TPU:1, one launch (start us, length us, event | category | flops | bytes accessed | tf_op | source)
XLA Modules:
  0.0 84.3 jit_solution(15079615350092461065)
XLA Ops:
  0.6 81.6 %shard_map.94 = (bf16[128,1280]{1,0:T(8,128)(2,1)S(1)}, bf16[6,128]{1,0:T(8,128)(2,1)S(1)}, f32[1,1280,768]{2,1,0:T(8,128)S(1)}) custom-call(s32[6,128]{1,0:T(8,128)} %bitcast.3, f32[6,128]{1,0:T(8,128)} %bitcast.4, bf16[128,1280]{1,0:T(8,128)(2,1)} %og_ref.1, bf16[1,576,2560]{2,1,0:T(8,128)(2,1)} %sin_hbm.1, bf16[1,1280,768]{2,1,0:T(8,128)(2,1)} %gw_hbm.1, ...), custom_call_target="tpu_custom_call" | custom-call | tf_op jit(solution)/shard_map/pallas_call | solution.py:346
  82.2 2.1 %shard_map.95 = (bf16[128,1280]{1,0:T(8,128)(2,1)}, bf16[6,128]{1,0:T(8,128)(2,1)}, f32[1,1280,768]{2,1,0:T(8,128)}) custom-call(bf16[128,1280]{1,0:T(8,128)(2,1)S(1)} %get-tuple-element.9.ig_ref, bf16[6,128]{1,0:T(8,128)(2,1)S(1)} %get-tuple-element.10.gg_ref, f32[1,1280,768]{2,1,0:T(8,128)S(1)} %get-tuple-element.11.dg_ref), custom_call_target="tpu_custom_call" | custom-call | tf_op jit(solution)/shard_map/pallas_call | solution.py:399

commit v4 on v3

--- a/solution.py
+++ b/solution.py
@@ -33,9 +33,10 @@
 def kernel(
     ids_ref, prob_ref, og_ref, sin_hbm, gw_hbm, uw_hbm, dw_hbm,
     ig_ref, gg_ref, dgv,
-    msg, over, recv, recvo, xs, sin, xin, wg, wu, wd, bm, cm, hid, pown, psend, precv, gpg, upg,
-    msg2, over2, rec2, rec2o, wmain, wovf, gm, acc, sref, stref, ptref,
-    lsem, wsem, hsem, psem, ssem, rsem, ssem2, rsem2, met,
+    ag0, ag1, ag2, idp, idpg, lhs, msg0, msg1, msg2_, over0, over1, over2_,
+    got0, got1, got2, goto0, goto1, goto2, xs, sin, xin, wg, wu, wd, bm, cm, hid, pown, psend, precv, gpg, upg,
+    msg2, over2, rec2, rec2o, wmain, wovf, gm, acc, sref, stref,
+    lsem, wsem, hsem, psem, ssem, rsem, ssem2, rsem2, asem, bsem,
 ):
     me = lax.axis_index("expert")
     f = lax.axis_index("fsdp")
@@ -54,55 +55,136 @@
 
     barrier = pltpu.get_barrier_semaphore()
 
-    def greet(i, carry):
-        d = near(me, f, 1 + 2 * (i % 2), i // 2)
-        pl.semaphore_signal(barrier, inc=1, device_id=(d, f), device_id_type=MESH)
-        return carry
-
-    lax.fori_loop(0, 32, greet, 0)
+    y, x = (me // 4) % 4, me % 4
+    mine = (z, y, x)
+    step_of = (PL, 4, 1)
+    spans = ((0, 512), (512, 896), (896, 1280))
+    gathered, sent, sent_over = (ag0, ag1, ag2), (msg0, msg1, msg2_), (over0, over1, over2_)
+    got, got_over = (got0, got1, got2), (goto0, goto1, goto2)
+
+    def mate(a, d):
+        return me + (((mine[a] + d) % 4) - mine[a]) * step_of[a]
+
+    for a in range(3):
+        for d in (1, 2, 3):
+            pl.semaphore_signal(barrier, inc=1, device_id=(mate(a, d), f), device_id_type=MESH)
     pl.semaphore_signal(barrier, inc=1, device_id=(me, 1 - f), device_id_type=MESH)
 
+    idp[...] = jnp.zeros_like(idp)
+    idp[0:top, :] = ids_ref[...].astype(F32)
+    idp[8 : 8 + top, :] = prob_ref[...]
+    for a, (lo, hi) in enumerate(spans):
+        gathered[a][mine[a]] = og_ref[:, lo:hi]
+        idpg[a, mine[a]] = idp[...]
     lane = iota((128, 128), 1)
     row = iota((128, 128), 0)
-    names = jnp.zeros((128, 128), F32)
-    probs = jnp.zeros((128, 128), F32)
-    for k in range(top):
-        hit = ids_ref[k : k + 1, :] == row
-        names = names + hit.astype(F32)
-        probs = probs + jnp.where(hit, prob_ref[k : k + 1, :], 0.0)
     before = (row < lane).astype(BF16)
-    rank = jnp.dot(names.astype(BF16), before, preferred_element_type=F32)
-    stref[...] = jnp.where(names > 0.0, rank, -1.0)
-    ptref[...] = probs
+
+    def line_copy(k, a, d):
+        lo, hi = spans[a]
+        src, dst = ((idp, idpg.at[a, mine[a]]), (og_ref.at[:, lo:hi], gathered[a].at[mine[a]]))[k]
+        return pltpu.make_async_remote_copy(
+            src_ref=src, dst_ref=dst, send_sem=asem.at[k, a], recv_sem=bsem.at[k, a],
+            device_id=(mate(a, d), f), device_id_type=MESH,
+        )
+
+    pl.semaphore_wait(barrier, 10)
+    for a in range(3):
+        for d in (1, 3, 2):
+            line_copy(0, a, d).start()
+    for d in (2, 1, 3):
+        for a in range(3):
+            line_copy(1, a, d).start()
 
     def place(r):
         main = r < PL * MAIN
         rest = r - PL * MAIN
         return jnp.where(main, r // MAIN, rest // REST), jnp.where(main, r % MAIN, MAIN + rest % REST)
 
-    def build(g):
-        who, slot = place(iota((G, 128), 0))
-        spread = (who + PL * g == iota((G, 128), 1)).astype(BF16)
-        s_rep = jnp.dot(spread, stref[...].astype(BF16), preferred_element_type=F32)
-        p_rep = jnp.dot(spread, ptref[...].astype(BF16), preferred_element_type=F32)
-        lhs = jnp.where(s_rep == slot.astype(F32), p_rep, 0.0).astype(BF16)
-        for n in range(0, feat, 256):
-            rows = jnp.dot(lhs, og_ref[:, n : n + 256], preferred_element_type=F32).astype(BF16)
-            msg[pl.ds(PL * g, PL), :, n : n + 256] = rows[0 : PL * MAIN].reshape(PL, MAIN, 256)
-            over[pl.ds(PL * g, PL), :, n : n + 256] = rows[PL * MAIN : G].reshape(PL, REST, 256)
+    def place_tokens(a, b):
+        table = idpg[a, b]
+        p = iota((PL, 128), 0)
+        u, v = p // 4, p % 4
+        expert = (PL * z + p, PL * u + 4 * y + v, PL * u + 4 * v + x)[a].astype(F32)
+        names = jnp.zeros((PL, 128), F32)
+        probs = jnp.zeros((PL, 128), F32)
+        for k in range(top):
+            hit = table[k : k + 1, :] == expert
+            names = names + hit.astype(F32)
+            probs = probs + jnp.where(hit, table[8 + k : 9 + k, :], 0.0)
+        rank = jnp.dot(names.astype(BF16), before, preferred_element_type=F32)
+        st = jnp.where(names > 0.0, rank, -1.0).astype(BF16)
+        who, _ = place(iota((G, PL), 0))
+        _, slot = place(iota((G, 128), 0))
+        spread = (who == iota((G, PL), 1)).astype(BF16)
+        s_rep = jnp.dot(spread, st, preferred_element_type=F32)
+        p_rep = jnp.dot(spread, probs.astype(BF16), preferred_element_type=F32)
+        lhs[a, b] = jnp.where(s_rep == slot.astype(F32), p_rep, 0.0).astype(BF16)
+
+    def build(a, b):
+        rows = jnp.dot(lhs[a, b], gathered[a][b], preferred_element_type=F32).astype(BF16)
+        wide = rows.shape[1]
+        main, rest = rows[0 : PL * MAIN], rows[PL * MAIN : G]
+        if a == 0:
+            sent[a][b % 2, :, b // 2] = main.reshape(PL, MAIN, wide)
+            sent_over[a][b % 2, :, b // 2] = rest.reshape(PL, REST, wide)
+        else:
+            sent[a][:, :, b] = main.reshape(4, 4, MAIN, wide)
+            sent_over[a][:, :, b] = rest.reshape(4, 4, REST, wide)
+
+    sign = 1 - 2 * f
 
     def dispatch(phase):
+        half = (z + 1 + phase) % 2
+
+        def plane_send(i, yx):
+            dy, dx = yx // 4, yx % 4
+            p = ((y + 4 + sign * dy) % 4) * 4 + (x + 4 + sign * dx) % 4
+            for k, (src, dst) in enumerate(((msg0, got0), (over0, goto0))):
+
+                @pl.when(yx == 0)
+                def _():
+                    pltpu.make_async_copy(src.at[half, p], dst.at[half, me % PL], rsem.at[k, 0, phase]).start()
+
+                @pl.when(yx != 0)
+                def _():
+                    pltpu.make_async_remote_copy(
+                        src_ref=src.at[half, p], dst_ref=dst.at[half, me % PL], send_sem=ssem.at[k, 0, phase],
+                        recv_sem=rsem.at[k, 0, phase], device_id=(z * PL + p, f), device_id_type=MESH,
+                    ).start()
+
+        def cross_send(i, a):
+            dz, dw = 1 - phase + 2 * (i % 2), i // 2
+            to_z = (z + 4 + sign * dz) % 4
+            w = mine[3 - a]
+            to_w = (w + 4 + sign * dw) % 4
+            d = to_z * PL + (y * 4 + to_w if a == 1 else to_w * 4 + x)
+            for k, (src, dst) in enumerate(((sent[a], got[a]), (sent_over[a], got_over[a]))):
+                there = dst.at[z % 2, z // 2, w]
+
+                def local():
+                    pltpu.make_async_copy(src.at[to_z, to_w], there, rsem.at[k, a, phase]).start()
+
+                def remote():
+                    pltpu.make_async_remote_copy(
+                        src_ref=src.at[to_z, to_w], dst_ref=there, send_sem=ssem.at[k, a, phase],
+                        recv_sem=rsem.at[k, a, phase], device_id=(d, f), device_id_type=MESH,
+                    ).start()
+
+                if phase == 0:
+                    remote()
+                else:
+                    pl.when(i == 0)(local)
+                    pl.when(i != 0)(remote)
+
         def step(i, carry):
-            j = (i * 5) % 32
-            d = near(me, f, 1 - phase + 2 * (j // PL), j % PL)
-            for b, (src, dst) in enumerate(((msg, recv), (over, recvo))):
-                pltpu.make_async_remote_copy(
-                    src_ref=src.at[d], dst_ref=dst.at[me], send_sem=ssem.at[b], recv_sem=rsem.at[b, z],
-                    device_id=(d, f), device_id_type=MESH,
-                ).start()
+            plane_send(i, (10 * i) % PL)
+            cross_send(i, 1)
+            plane_send(i, (10 * i + 5) % PL)
+            cross_send(i, 2)
             return carry
 
-        lax.fori_loop(phase, 32, step, 0)
+        lax.fori_loop(0, 8, step, 0)
 
     def weight_copies():
         return [
@@ -113,27 +195,29 @@
             for i, (h, w) in enumerate(((gw_hbm, wg), (uw_hbm, wu)))
         ]
 
-    def build_odd(i, carry):
-        build((z + 1 + 2 * i) % 4)
-        return carry
-
-    lax.fori_loop(0, 2, build_odd, 0)
-    pl.semaphore_wait(barrier, 33)
-    pl.semaphore_signal(met.at[0], inc=1, device_id=((me + PL) % E, f), device_id_type=MESH)
-    dispatch(0)
     for c in weight_copies():
         c.start()
-
-    def build_even(i, carry):
-        build((z + 2 * i) % 4)
-        return carry
-
-    lax.fori_loop(0, 2, build_even, 0)
-    pl.semaphore_wait(met.at[0], 1)
-    pl.semaphore_signal(met.at[1], inc=1, device_id=(me, 1 - f), device_id_type=MESH)
+    def line_wait(k, refs):
+        for a, ref in enumerate(refs):
+            three = ref.at[pl.ds(0, 3)]
+            pltpu.make_async_copy(three, three, bsem.at[k, a]).wait()
+
+    line_wait(0, [idpg.at[a] for a in range(3)])
+    for a in range(3):
+        for b in range(4):
+            place_tokens(a, b)
+    line_wait(1, gathered)
+    for a in range(3):
+        for b in range(4):
+            build(a, b)
+    dispatch(0)
     dispatch(1)
-    pltpu.make_async_copy(msg.at[me], recv.at[me], rsem.at[0, z]).start()
-    pltpu.make_async_copy(over.at[me], recvo.at[me], rsem.at[1, z]).start()
+
+    names = jnp.zeros((128, 128), F32)
+    for k in range(top):
+        names = names + (ids_ref[k : k + 1, :] == row).astype(F32)
+    rank = jnp.dot(names.astype(BF16), before, preferred_element_type=F32)
+    stref[...] = jnp.where(names > 0.0, rank, -1.0)
 
     sref[...] = stref[...].T
     s_half = sref[...].astype(BF16)
@@ -190,10 +274,26 @@
             slab = ref.at[pl.ds(PL * g, PL)]
             pltpu.make_async_copy(slab, slab, sems.at[b, g]).wait()
 
-    def unpack(g):
-        arrived((recv, recvo), rsem, g)
-        xs[g, 0 : PL * MAIN, :] = recv[pl.ds(PL * g, PL)].reshape(PL * MAIN, feat)
-        xs[g, PL * MAIN : G, :] = recvo[pl.ds(PL * g, PL)].reshape(PL * REST, feat)
+    def wait_phase(phase, half):
+        for a in range(3):
+            for k, ref in enumerate((got[a], got_over[a])):
+                pltpu.make_async_copy(ref.at[half], ref.at[half], rsem.at[k, a, phase]).wait()
+
+    def unpack(half, top_half):
+        g = 2 * top_half + half
+        n = PL * MAIN
+        for a, (lo, hi) in enumerate(spans):
+            if a == 0:
+                xs[g, 0:n, lo:hi] = got[a][half, :, top_half].reshape(n, hi - lo)
+                xs[g, n:G, lo:hi] = got_over[a][half, :, top_half].reshape(G - n, hi - lo)
+            elif a == 1:
+                for b in range(4):
+                    xs[g, 64 * b : 64 * b + 64, lo:hi] = got[a][half, top_half, :, b].reshape(64, hi - lo)
+                rest = jnp.concatenate([got_over[a][half, top_half, :, b] for b in range(4)], axis=0)
+                xs[g, n:G, lo:hi] = rest.reshape(G - n, hi - lo)
+            else:
+                xs[g, 0:n, lo:hi] = got[a][half, top_half].reshape(n, hi - lo)
+                xs[g, n:G, lo:hi] = got_over[a][half, top_half].reshape(G - n, hi - lo)
 
     def partial_copy(q):
         return pltpu.make_async_remote_copy(
@@ -203,10 +303,11 @@
 
     def back(i, carry):
         q = (z + 1 + i) % 2
-        unpack(2 * (1 - f) + q)
+        wait_phase(i, q)
+        unpack(q, 1 - f)
         psend[q] = jnp.dot(xs[2 * (1 - f) + q], wd[...], preferred_element_type=F32)
         partial_copy(q).start()
-        unpack(2 * f + q)
+        unpack(q, f)
         pown[...] = jnp.dot(xs[2 * f + q], wd[...], preferred_element_type=F32)
         partial_copy(q).wait_recv()
         raw = pown[...] + precv[q]
@@ -234,7 +335,7 @@
                 over2[q, h, :, :, n : n + 256] = rows[PL * MAIN : G].reshape(PL, REST, 256)
 
             def send(j, carry):
-                blk = near((2 * f + q) * PL + me % PL, f, 0, (j * 5) % PL)
+                blk = near((2 * f + q) * PL + me % PL, f, 0, (j * 7) % PL)
                 here = jnp.logical_and(blk == me, h == f)
 
                 for b, (src, dst) in enumerate(((msg2, rec2), (over2, rec2o))):
@@ -255,7 +356,6 @@
             lax.fori_loop(0, PL, send, 0)
         return carry
 
-    pl.semaphore_wait(met.at[1], 1)
     lax.fori_loop(0, 2, back, 0)
 
     hid_copy.wait()
@@ -300,9 +400,18 @@
         values = jnp.where(row[0:8] == k, value, values)
     gg_ref[...] = values[0:top].astype(BF16)
 
-    for b, ref in enumerate((msg, over)):
-        most = ref.at[pl.ds(0, E - 1)]
-        pltpu.make_async_copy(most, most, ssem.at[b]).wait()
+    for a in range(3):
+        for k, ref in enumerate((idpg.at[a], gathered[a])):
+            three = ref.at[pl.ds(0, 3)]
+            pltpu.make_async_copy(three, three, asem.at[k, a]).wait()
+        for phase in range(2):
+            for k, ref in enumerate((sent[a], sent_over[a])):
+                if a == 0:
+                    most = ref.at[0, pl.ds(0, PL - 1)]
+                    pltpu.make_async_copy(most, most, ssem.at[k, a, phase]).wait()
+                else:
+                    for part in (ref.at[0], ref.at[1] if phase == 0 else ref.at[1, pl.ds(0, 3)]):
+                        pltpu.make_async_copy(part, part, ssem.at[k, a, phase]).wait()
     for q in range(2):
         partial_copy(q).wait_send()
         for h in range(2):
@@ -353,10 +462,24 @@
         in_specs=[vmem, vmem, vmem, hbm, hbm, hbm, hbm],
         out_specs=(vmem, vmem, vmem),
         scratch_shapes=[
-            pltpu.VMEM((E, MAIN, feat), BF16),
-            pltpu.VMEM((E, REST, feat), BF16),
-            pltpu.VMEM((E, MAIN, feat), BF16),
-            pltpu.VMEM((E, REST, feat), BF16),
+            pltpu.VMEM((4, tokens, 512), BF16),
+            pltpu.VMEM((4, tokens, 384), BF16),
+            pltpu.VMEM((4, tokens, 384), BF16),
+            pltpu.VMEM((16, tokens), F32),
+            pltpu.VMEM((3, 4, 16, tokens), F32),
+            pltpu.VMEM((3, 4, G, tokens), BF16),
+            pltpu.VMEM((2, PL, 2, MAIN, 512), BF16),
+            pltpu.VMEM((4, 4, 4, MAIN, 384), BF16),
+            pltpu.VMEM((4, 4, 4, MAIN, 384), BF16),
+            pltpu.VMEM((2, PL, 2, REST, 512), BF16),
+            pltpu.VMEM((4, 4, 4, REST, 384), BF16),
+            pltpu.VMEM((4, 4, 4, REST, 384), BF16),
+            pltpu.VMEM((2, PL, 2, MAIN, 512), BF16),
+            pltpu.VMEM((2, 2, 4, 4, MAIN, 384), BF16),
+            pltpu.VMEM((2, 2, 4, 4, MAIN, 384), BF16),
+            pltpu.VMEM((2, PL, 2, REST, 512), BF16),
+            pltpu.VMEM((2, 2, 4, 4, REST, 384), BF16),
+            pltpu.VMEM((2, 2, 4, 4, REST, 384), BF16),
             pltpu.VMEM((4, G, feat), BF16),
             pltpu.VMEM((2 * G, 2 * feat), BF16),
             pltpu.VMEM((2, G, 2 * feat), BF16),
@@ -381,16 +504,16 @@
             pltpu.VMEM((tokens, feat), F32),
             pltpu.VMEM((tokens, 128), F32),
             pltpu.VMEM((128, tokens), F32),
-            pltpu.VMEM((128, tokens), F32),
             dma((4,)),
             dma((2, 2)),
             dma((2,)),
             dma((2, 2)),
-            dma((2,)),
-            dma((2, 4)),
+            dma((2, 3, 2)),
+            dma((2, 3, 2)),
             dma((2, 2, 2)),
             dma((2, 4)),
-            pltpu.SemaphoreType.REGULAR((2,)),
+            dma((2, 3)),
+            dma((2, 3)),
         ],
         compiler_params=pltpu.CompilerParams(
             collective_id=0, has_side_effects=True, vmem_limit_bytes=50 << 20

time: 84.5 us -> 79.3 us (0.938)
  Pallas kernels: 83.7 us -> 78.5 us
    pallas_call x1, Pallas kernels: 81.6 us -> 76.5 us  [body(): pl.pallas_call(kernel, out_shape=(pltpu.VMEM((tokens, feat), BF16), pltpu...]
where the time goes in v4:
time: 79.3 us; the launch traced here: 79.2 us
  Pallas kernels  78.5 us (99%)
    pallas_call x1, Pallas kernels, body(): pl.pallas_call(kernel, out_shape=(pltpu.VMEM((tokens, feat), BF16), pltpu...  76.5 us
    pallas_call x1, Pallas kernels, body(): pl.pallas_call(flush, out_shape=(pltpu.HBM((tokens, feat), BF16), pltpu.H...  2.07 us

profile of v4, /device:TPU:1, one launch (start us, length us, event | category | flops | bytes accessed | tf_op | source)
XLA Modules:
  0.0 79.2 jit_solution(13352639757395206081)
XLA Ops:
  0.6 76.5 %shard_map.94 = (bf16[128,1280]{1,0:T(8,128)(2,1)S(1)}, bf16[6,128]{1,0:T(8,128)(2,1)S(1)}, f32[1,1280,768]{2,1,0:T(8,128)S(1)}) custom-call(s32[6,128]{1,0:T(8,128)} %bitcast.3, f32[6,128]{1,0:T(8,128)} %bitcast.4, bf16[128,1280]{1,0:T(8,128)(2,1)} %og_ref.1, bf16[1,576,2560]{2,1,0:T(8,128)(2,1)} %sin_hbm.1, bf16[1,1280,768]{2,1,0:T(8,128)(2,1)} %gw_hbm.1, ...), custom_call_target="tpu_custom_call" | custom-call | tf_op jit(solution)/shard_map/pallas_call | solution.py:455
  77.1 2.1 %shard_map.95 = (bf16[128,1280]{1,0:T(8,128)(2,1)}, bf16[6,128]{1,0:T(8,128)(2,1)}, f32[1,1280,768]{2,1,0:T(8,128)}) custom-call(bf16[128,1280]{1,0:T(8,128)(2,1)S(1)} %get-tuple-element.9.ig_ref, bf16[6,128]{1,0:T(8,128)(2,1)S(1)} %get-tuple-element.10.gg_ref, f32[1,1280,768]{2,1,0:T(8,128)S(1)} %get-tuple-element.11.dg_ref), custom_call_target="tpu_custom_call" | custom-call | tf_op jit(solution)/shard_map/pallas_call | solution.py:522

commit v5 on v4

--- a/solution.py
+++ b/solution.py
@@ -207,10 +207,14 @@
         for b in range(4):
             place_tokens(a, b)
     line_wait(1, gathered)
-    for a in range(3):
+    for a in (1, 2):
         for b in range(4):
             build(a, b)
+    for t in range(2):
+        build(0, 2 * t + (z + 1) % 2)
     dispatch(0)
+    for t in range(2):
+        build(0, 2 * t + z % 2)
     dispatch(1)
 
     names = jnp.zeros((128, 128), F32)

time: 79.3 us -> 79 us (level)
  no operation moved by 1% of the time
where the time goes in v5:
time: 79 us; the launch traced here: 78.9 us
  Pallas kernels  78.3 us (99%)
    pallas_call x1, Pallas kernels, body(): pl.pallas_call(kernel, out_shape=(pltpu.VMEM((tokens, feat), BF16), pltpu...  76.2 us
    pallas_call x1, Pallas kernels, body(): pl.pallas_call(flush, out_shape=(pltpu.HBM((tokens, feat), BF16), pltpu.H...  2.07 us

profile of v5, /device:TPU:1, one launch (start us, length us, event | category | flops | bytes accessed | tf_op | source)
XLA Modules:
  0.0 78.9 jit_solution(2351767441786201022)
XLA Ops:
  0.6 76.2 %shard_map.94 = (bf16[128,1280]{1,0:T(8,128)(2,1)S(1)}, bf16[6,128]{1,0:T(8,128)(2,1)S(1)}, f32[1,1280,768]{2,1,0:T(8,128)S(1)}) custom-call(s32[6,128]{1,0:T(8,128)} %bitcast.3, f32[6,128]{1,0:T(8,128)} %bitcast.4, bf16[128,1280]{1,0:T(8,128)(2,1)} %og_ref.1, bf16[1,576,2560]{2,1,0:T(8,128)(2,1)} %sin_hbm.1, bf16[1,1280,768]{2,1,0:T(8,128)(2,1)} %gw_hbm.1, ...), custom_call_target="tpu_custom_call" | custom-call | tf_op jit(solution)/shard_map/pallas_call | solution.py:459
  76.8 2.1 %shard_map.95 = (bf16[128,1280]{1,0:T(8,128)(2,1)}, bf16[6,128]{1,0:T(8,128)(2,1)}, f32[1,1280,768]{2,1,0:T(8,128)}) custom-call(bf16[128,1280]{1,0:T(8,128)(2,1)S(1)} %get-tuple-element.9.ig_ref, bf16[6,128]{1,0:T(8,128)(2,1)S(1)} %get-tuple-element.10.gg_ref, f32[1,1280,768]{2,1,0:T(8,128)S(1)} %get-tuple-element.11.dg_ref), custom_call_target="tpu_custom_call" | custom-call | tf_op jit(solution)/shard_map/pallas_call | solution.py:526
